TPU v7x, 256 devices: a whole 4x4x8 slice. The times are simulated.
256 devices in a mesh: shot: 8 (over x, y_lo), domain: 32 (over z, y_hi, core).
Axes of the slice: x: 4, y: 4 (y_hi: 2, y_lo: 2; y = y_hi * 2 + y_lo), z: 8, core: 2. Of those that a mesh axis runs over, the one named last changes fastest.
Arguments:
- velsq: float32 [64, 256, 128], P('domain', 'shot'), may hold values from 0.04 to 0.12
- epsilon: float32 [64, 256, 128], P('domain', 'shot'), may hold values from 0 to 0.3
- delta: float32 [64, 256, 128], P('domain', 'shot'), may hold values from 0 to 0.15
- tilt: float32 [64, 256, 128], P('domain', 'shot'), may hold values from -1.2 to 1.2
- azimuth: float32 [64, 256, 128], P('domain', 'shot'), may hold values from -3.140625 to 3.140625
- forward_state: float32 [8, 4, 64, 256, 128], P('shot', None, 'domain'), may hold values from -6 to 6
- adjoint_state: float32 [8, 4, 64, 256, 128], P('shot', None, 'domain'), may hold values from -6 to 6
- wavelet: float32 [8, 2], P('shot'), may hold values from -60 to 60
- source: int32 [8], P('shot'), may hold values from 0 to 2097151
- receivers: int32 [8, 256], P('shot'), may hold values from 0 to 2097151
- observed: float32 [8, 2, 256], P('shot'), may hold values from -18 to 18
Outputs:
- gradients: float32 [5, 64, 256, 128], P(None, 'domain', 'shot')
Inputs may be any that keep to these rules, and one draw needn't show every extreme that they name: `source`: flat index x * 256 * 128 + y * 128 + z of a grid cell. `receivers`: flat index x * 256 * 128 + y * 128 + z of a grid cell; cells may repeat.
All inputs are finite; a program needn't handle non-finite values.
Results may differ from a plain program's by a relative error of at most 0.0001.
Values sent between devices are 32-bit elements; how exact they have to be, the bound alone decides.
A program may use at most 128 MiB of HBM per device.

v0:
```python
import jax
import jax.numpy as jnp
from jax import lax
from jax.sharding import PartitionSpec as P

STEPS = 2


def with_halo(block, sides, width):
    for axis, dim in sides:
        count = lax.axis_size(axis)
        forward = [(i, i + 1) for i in range(count - 1)]
        backward = [(target, source) for source, target in forward]
        low = lax.ppermute(
            lax.slice_in_dim(block, block.shape[dim] - width, None, axis=dim), axis, forward
        )
        high = lax.ppermute(lax.slice_in_dim(block, 0, width, axis=dim), axis, backward)
        block = jnp.concatenate([low, block, high], axis=dim)
    return block


def hessian(values):
    padded = jnp.pad(values, ((0, 0), (1, 1), (1, 1)))
    center = padded[1:-1, 1:-1, 1:-1]
    curve_xx = padded[2:, 1:-1, 1:-1] + padded[:-2, 1:-1, 1:-1] - 2.0 * center
    curve_yy = padded[1:-1, 2:, 1:-1] + padded[1:-1, :-2, 1:-1] - 2.0 * center
    curve_zz = padded[1:-1, 1:-1, 2:] + padded[1:-1, 1:-1, :-2] - 2.0 * center
    mixed_xy = 0.25 * (
        padded[2:, 2:, 1:-1]
        - padded[2:, :-2, 1:-1]
        - padded[:-2, 2:, 1:-1]
        + padded[:-2, :-2, 1:-1]
    )
    mixed_xz = 0.25 * (
        padded[2:, 1:-1, 2:]
        - padded[2:, 1:-1, :-2]
        - padded[:-2, 1:-1, 2:]
        + padded[:-2, 1:-1, :-2]
    )
    mixed_yz = 0.25 * (
        padded[1:-1, 2:, 2:]
        - padded[1:-1, 2:, :-2]
        - padded[1:-1, :-2, 2:]
        + padded[1:-1, :-2, :-2]
    )
    return jnp.stack([curve_xx, curve_yy, curve_zz, mixed_xy, mixed_xz, mixed_yz])


def tables(velsq, epsilon, delta, tilt, azimuth):
    sin_tilt = jnp.sin(tilt)
    cos_tilt = jnp.cos(tilt)
    sin_azim = jnp.sin(azimuth)
    cos_azim = jnp.cos(azimuth)
    axis_x = sin_tilt * cos_azim
    axis_y = sin_tilt * sin_azim
    turn_x = cos_tilt * cos_azim
    turn_y = cos_tilt * sin_azim
    turn_z = -sin_tilt
    spin_x = -sin_tilt * sin_azim
    spin_y = sin_tilt * cos_azim
    along = jnp.stack(
        [
            axis_x * axis_x,
            axis_y * axis_y,
            cos_tilt * cos_tilt,
            2.0 * axis_x * axis_y,
            2.0 * axis_x * cos_tilt,
            2.0 * axis_y * cos_tilt,
        ]
    )
    by_tilt = jnp.stack(
        [
            2.0 * turn_x * axis_x,
            2.0 * turn_y * axis_y,
            2.0 * turn_z * cos_tilt,
            2.0 * (turn_x * axis_y + turn_y * axis_x),
            2.0 * (turn_x * cos_tilt + turn_z * axis_x),
            2.0 * (turn_y * cos_tilt + turn_z * axis_y),
        ]
    )
    by_spin = jnp.stack(
        [
            2.0 * spin_x * axis_x,
            2.0 * spin_y * axis_y,
            jnp.zeros_like(cos_tilt),
            2.0 * (spin_x * axis_y + spin_y * axis_x),
            2.0 * spin_x * cos_tilt,
            2.0 * spin_y * cos_tilt,
        ]
    )
    return (velsq, 1.0 + 2.0 * epsilon, jnp.sqrt(1.0 + 2.0 * delta), along, by_tilt, by_spin)


def operate(pad_p, pad_q, table, full):
    speed_sq, stretch, root_d, along, by_tilt, by_spin = table
    hess_p = hessian(pad_p)
    hess_q = hessian(pad_q)
    laplace = hess_p[0] + hess_p[1] + hess_p[2]
    axial_p = jnp.sum(along * hess_p, axis=0)
    axial_q = jnp.sum(along * hess_q, axis=0)
    across = laplace - axial_p
    drive_p = stretch * across + root_d * axial_q
    drive_q = root_d * across + axial_q
    if full:
        image_terms = (
            across,
            axial_q,
            jnp.sum(by_tilt * hess_p, axis=0),
            jnp.sum(by_tilt * hess_q, axis=0),
            jnp.sum(by_spin * hess_p, axis=0),
            jnp.sum(by_spin * hess_q, axis=0),
        )
        return (drive_p, drive_q, image_terms)
    return (drive_p, drive_q, ())


def advance(pad_p, pad_q, prior_p, prior_q, table, full):
    drive_p, drive_q, image_terms = operate(pad_p, pad_q, table, full)
    speed_sq = table[0]
    next_p = 2.0 * pad_p[1:-1] - prior_p + speed_sq * drive_p
    next_q = 2.0 * pad_q[1:-1] - prior_q + speed_sq * drive_q
    return (next_p, next_q, image_terms)


def correlate(gradient, adjoint_p, adjoint_q, image_terms, table):
    speed_sq, stretch, root_d, along, by_tilt, by_spin = table
    across, axial_q, tilt_p, tilt_q, spin_p, spin_q = image_terms
    g_speed = (
        gradient[0]
        + adjoint_p * (stretch * across + root_d * axial_q)
        + adjoint_q * (root_d * across + axial_q)
    )
    g_eps = gradient[1] + 2.0 * speed_sq * adjoint_p * across
    g_delta = gradient[2] + speed_sq * (adjoint_p * axial_q + adjoint_q * across) / root_d
    g_tilt = gradient[3] + speed_sq * (
        adjoint_p * (root_d * tilt_q - stretch * tilt_p) + adjoint_q * (tilt_q - root_d * tilt_p)
    )
    g_spin = gradient[4] + speed_sq * (
        adjoint_p * (root_d * spin_q - stretch * spin_p) + adjoint_q * (spin_q - root_d * spin_p)
    )
    return (g_speed, g_eps, g_delta, g_tilt, g_spin)


def inject(values, start_row, target, amount):
    layout = values.shape
    plane_size = layout[1] * layout[2]
    offset = target - start_row * plane_size
    inside = (offset >= 0) & (offset < layout[0] * plane_size)
    clipped = jnp.where(inside, offset, 0)
    return values.reshape(-1).at[clipped].add(jnp.where(inside, amount, 0.0)).reshape(layout)


def sample_cells(values, start_row, target):
    layout = values.shape
    plane_size = layout[1] * layout[2]
    offset = target - start_row * plane_size
    inside = (offset >= 0) & (offset < layout[0] * plane_size)
    clipped = jnp.where(inside, offset, 0)
    return jnp.where(inside, values.reshape(-1)[clipped], 0.0)


def single_rim(field_p, field_q):
    padded = with_halo(jnp.stack([field_p, field_q]), (("domain", 1),), 1)
    return (padded[0], padded[1])


def shards(
    velsq,
    epsilon,
    delta,
    tilt,
    azimuth,
    forward_state,
    adjoint_state,
    wavelet,
    source,
    receivers,
    observed,
):
    gathered = (
        lax.all_gather(velsq, "shot", axis=1, tiled=True),
        lax.all_gather(epsilon, "shot", axis=1, tiled=True),
        lax.all_gather(delta, "shot", axis=1, tiled=True),
        lax.all_gather(tilt, "shot", axis=1, tiled=True),
        lax.all_gather(azimuth, "shot", axis=1, tiled=True),
    )
    row_count = gathered[0].shape[0]
    first_row = lax.axis_index("domain") * row_count
    inner = tables(gathered[0], gathered[1], gathered[2], gathered[3], gathered[4])
    full_terms = False
    full_terms = True
    source_cell = source[0]
    receiver_cells = receivers[0]
    older_p, field_p, older_q, field_q = (
        forward_state[0, 0],
        forward_state[0, 1],
        forward_state[0, 2],
        forward_state[0, 3],
    )
    saved = []
    traces = []
    for moment in range(STEPS):
        pad_p, pad_q = single_rim(field_p, field_q)
        next_p, next_q, image_terms = advance(pad_p, pad_q, older_p, older_q, inner, full_terms)
        next_p = inject(next_p, first_row, source_cell, wavelet[0, moment])
        next_q = inject(next_q, first_row, source_cell, wavelet[0, moment])
        saved.append(image_terms)
        traces.append(sample_cells(next_p, first_row, receiver_cells))
        older_p, field_p, older_q, field_q = (field_p, next_p, field_q, next_q)
    recorded = lax.psum(jnp.stack(traces), "domain")
    misfit = recorded - observed[0]
    gradient = tuple((jnp.zeros(field_p.shape, jnp.float32) for member in range(5)))
    before_p, adjoint_p, before_q, adjoint_q = (
        adjoint_state[0, 0],
        adjoint_state[0, 1],
        adjoint_state[0, 2],
        adjoint_state[0, 3],
    )
    for moment in range(STEPS):
        back_index = STEPS - 1 - moment
        gradient = correlate(gradient, adjoint_p, adjoint_q, saved[back_index], inner)
        pad_p, pad_q = single_rim(adjoint_p, adjoint_q)
        next_p, next_q, unused = advance(pad_p, pad_q, before_p, before_q, inner, False)
        next_p = inject(next_p, first_row, receiver_cells, misfit[back_index])
        before_p, adjoint_p, before_q, adjoint_q = (adjoint_p, next_p, adjoint_q, next_q)
    return lax.psum_scatter(jnp.stack(gradient), "shot", scatter_dimension=2, tiled=True)


def solution(mesh):
    placed = (
        P("domain", "shot", None),
        P("domain", "shot", None),
        P("domain", "shot", None),
        P("domain", "shot", None),
        P("domain", "shot", None),
        P("shot", None, "domain", None, None),
        P("shot", None, "domain", None, None),
        P("shot", None),
        P("shot"),
        P("shot", None),
        P("shot", None, None),
    )
    return jax.shard_map(
        shards,
        mesh=mesh,
        in_specs=placed,
        out_specs=P(None, "domain", "shot", None),
        check_vma=False,
    )
```

profile of v0, /device:TPU:48, one launch (start us, length us, event | category | flops | bytes accessed | tf_op | source)
XLA Modules:
  0.0 353.9 jit_solution(16403042310096619500)
XLA Ops:
  6.5 1.2 slice_bitcast_fusion.9
  8.5 1.9 collective-permute-start.4
  10.4 2.4 collective-permute-start.5
  12.9 0.8 fusion.2
  13.7 4.8 %collective-permute-start = (f32[2,1,256,128]{3,2,1,0:T(8,128)}, f32[2,1,256,128]{3,2,1,0:T(8,128)}, u32[]{:S(2)}, u32[]{:S(2)}) collective-permute-start(f32[2,1,256,128]{3,2,1,0:T(8,128)} %get-tuple-element.99), channel_id=1, source_target_pairs={{1,0},{2,1},{3,2},{4,3},{5,4},{6,5},{7,6},{8,7},{9,8},{10,9},{11,1... | collective-permute-start | bytes 786440 | tf_op jit(solution)/shard_map/ppermute | solution.py:17
  18.5 2.6 collective-permute-start.1
  21.2 28.6 %all_gather.17 = f32[2,256,128]{2,1,0:T(8,128)S(1)} all-gather(f32[2,32,128]{2,1,0:T(8,128)S(1)} %copy-done.35), channel_id=1, replica_groups=mesh['shot'=8,'domain'=32] {'shot'}, dimensions={1}, use_global_device_ids=true | all-gather | bytes 294912 | tf_op jit(solution)/shard_map/all_gather | solution.py:184
  49.8 0.9 fusion.194
  50.8 28.6 %all_gather.18 = f32[2,256,128]{2,1,0:T(8,128)S(1)} all-gather(f32[2,32,128]{2,1,0:T(8,128)S(1)} %copy-done.36), channel_id=1, replica_groups=mesh['shot'=8,'domain'=32] {'shot'}, dimensions={1}, use_global_device_ids=true | all-gather | bytes 294912 | tf_op jit(solution)/shard_map/all_gather | solution.py:185
  79.4 0.9 fusion.193
  80.4 28.4 %all_gather.16 = f32[2,256,128]{2,1,0:T(8,128)S(1)} all-gather(f32[2,32,128]{2,1,0:T(8,128)S(1)} %copy-done.37), channel_id=1, replica_groups=mesh['shot'=8,'domain'=32] {'shot'}, dimensions={1}, use_global_device_ids=true | all-gather | bytes 294912 | tf_op jit(solution)/shard_map/all_gather | solution.py:181
  108.8 28.4 %all_gather.19 = f32[2,256,128]{2,1,0:T(8,128)S(1)} all-gather(f32[2,32,128]{2,1,0:T(8,128)S(1)} %copy-done.38), channel_id=1, replica_groups=mesh['shot'=8,'domain'=32] {'shot'}, dimensions={1}, use_global_device_ids=true | all-gather | bytes 294912 | tf_op jit(solution)/shard_map/all_gather | solution.py:183
  137.2 28.4 %all_gather.15 = f32[2,256,128]{2,1,0:T(8,128)S(1)} all-gather(f32[2,32,128]{2,1,0:T(8,128)S(1)} %copy-done.39), channel_id=1, replica_groups=mesh['shot'=8,'domain'=32] {'shot'}, dimensions={1}, use_global_device_ids=true | all-gather | bytes 294912 | tf_op jit(solution)/shard_map/all_gather | solution.py:182
  167.0 0.9 bitcast_dynamic-update-slice_fusion.9
  167.9 0.9 bitcast_dynamic-update-slice_fusion.26
  168.8 1.0 bitcast_dynamic-update-slice_fusion.8
  169.8 0.9 bitcast_dynamic-update-slice_fusion.7
  170.7 0.9 bitcast_dynamic-update-slice_fusion.6
  171.6 1.0 bitcast_dynamic-update-slice_fusion.5
  175.3 1.1 pad_maximum_fusion.2
  176.5 1.1 copy-done
  177.7 1.9 subtract_dynamic-update-slice_fusion
  179.7 0.9 bitcast_dynamic-update-slice_fusion.14
  180.6 0.9 fusion.108
  182.3 1.5 pad_maximum_fusion
  183.9 1.1 fusion.155
  185.1 1.1 fusion.28
  188.2 2.4 multiply_reduce_fusion.13
  190.7 1.4 fusion.177
  194.9 1.9 collective-permute-start.2
  196.8 2.6 collective-permute-start.3
  200.3 1.7 gather_fusion
  202.0 1.1 fusion.140
  203.1 1.0 fusion.146
  204.1 4.2 %collective-permute-done.3 = f32[2,1,256,128]{3,2,1,0:T(8,128)} collective-permute-done((f32[2,1,256,128]{3,2,1,0:T(8,128)}, f32[2,1,256,128]{3,2,1,0:T(8,128)}, u32[]{:S(2)}, u32[]{:S(2)}) %collective-permute-start.3) | collective-permute-done | bytes 262176 | tf_op jit(solution)/shard_map/ppermute | solution.py:14
  208.3 1.1 pad_maximum_fusion.1
  209.5 1.2 fusion.152
  213.8 5.6 %multiply_reduce_fusion.2 = (f32[2,256,128]{2,1,0:T(8,128)}, f32[2,256,128]{2,1,0:T(8,128)}, f32[2,256,128]{2,1,0:T(8,128)}, f32[2,256,128]{2,1,0:T(8,128)}, f32...) fusion(f32[6,2,256,128]{3,2,1,0:T(8,128)} %bitcast_dynamic-upda, ...), kind=kLoop, calls=%fused_computation.101 | loop fusion | flops 8650752 | bytes 17301504 | tf_op jit(solution)/shard_map/reduce_sum | solution.py:110
  219.4 2.2 fusion.182
  221.8 1.7 gather_fusion.1
  223.5 55.7 %psum.7 = f32[2,256]{1,0:T(2,128)S(1)} all-reduce(f32[2,256]{1,0:T(2,128)S(1)} %pad_maximum_fusion.18), channel_id=1, replica_groups=mesh['shot'=8,'domain'=32] {'domain'}, use_global_device_ids=true, to_apply=%region_6.7 | all-reduce | flops 512 | bytes 4096 | tf_op jit(solution)/shard_map/psum | solution.py:210
  279.2 2.1 fusion.160
  281.4 2.4 scatter_fusion
  283.8 2.0 bitcast_dynamic-update-slice_fusion.13
  286.6 0.9 bitcast_dynamic-update-slice_fusion.11
  287.9 1.0 bitcast_dynamic-update-slice_fusion.4
  289.2 1.0 bitcast_dynamic-update-slice_fusion
  290.1 57.0 %reduce-scatter.2.cloned.1.call-done = f32[5,2,32,128]{3,2,1,0:T(8,128)} async-done(((f32[5,2,256,128]{3,2,1,0:T(8,128)}), f32[5,2,32,128]{3,2,1,0:T(8,128)}) %reduce-scatter.2.cloned.1.call-update) | async-done | bytes 163856 | tf_op jit(solution)/shard_map/reduce_scatter | solution.py:226
  (134 shorter events, 14.6 us)
Async XLA Ops:
  6.5 6.3 %copy-start.1 = (f32[1,4,2,256,128]{4,3,2,1,0:T(8,128)S(1)}, f32[1,4,2,256,128]{4,3,2,1,0:T(8,128)}, u32[]{:S(2)}) copy-start(f32[1,4,2,256,128]{4,3,2,1,0:T(8,128)} %param.22) | copy-start | bytes 3145732
  6.5 340.6 %reduce-scatter.2.cloned.1.call-start = ((), (), s32[]{:S(2)}) async-start(), calls=%async_computation.1 | async-start | bytes 1474560 | tf_op jit(solution)/shard_map/reduce_scatter | solution.py:226
  7.7 167.6 %copy-start.11 = (f32[1,2,256,128]{3,2,1,0:T(8,128)}, f32[1,2,256,128]{3,2,1,0:T(8,128)S(1)}, u32[]{:S(2)}) copy-start(f32[1,2,256,128]{3,2,1,0:T(8,128)S(1)} %get-tuple-element.73) | copy-start | bytes 786436
  7.7 167.6 %copy-start.14 = (f32[1,2,256,128]{3,2,1,0:T(8,128)}, f32[1,2,256,128]{3,2,1,0:T(8,128)S(1)}, u32[]{:S(2)}) copy-start(f32[1,2,256,128]{3,2,1,0:T(8,128)S(1)} %get-tuple-element.74) | copy-start | bytes 786436
  7.7 13.5 %copy-start.35 = (f32[2,32,128]{2,1,0:T(8,128)S(1)}, f32[2,32,128]{2,1,0:T(8,128)}, u32[]{:S(2)}) copy-start(f32[2,32,128]{2,1,0:T(8,128)} %param.20) | copy-start | bytes 98308
  8.5 166.8 %collective-permute-start.4 = (f32[2,1,256,128]{3,2,1,0:T(8,128)}, f32[2,1,256,128]{3,2,1,0:T(8,128)}, u32[]{:S(2)}, u32[]{:S(2)}) collective-permute-start(f32[2,1,256,128]{3,2,1,0:T(8,128)} %get-tuple-element.91), channel_id=1, source_target_pairs={{1,0},{2,1},{3,2},{4,3},{5,4},{6,5},{7,6},{8,7},{9,8},{10,9},{11,1... | collective-permute-start | bytes 786440 | tf_op jit(solution)/shard_map/ppermute | solution.py:17
  10.4 40.4 %copy-start.36 = (f32[2,32,128]{2,1,0:T(8,128)S(1)}, f32[2,32,128]{2,1,0:T(8,128)}, u32[]{:S(2)}) copy-start(f32[2,32,128]{2,1,0:T(8,128)} %param.21) | copy-start | bytes 98308
  10.4 164.9 %collective-permute-start.5 = (f32[2,1,256,128]{3,2,1,0:T(8,128)S(1)}, f32[2,1,256,128]{3,2,1,0:T(8,128)}, u32[]{:S(2)}, u32[]{:S(2)}) collective-permute-start(f32[2,1,256,128]{3,2,1,0:T(8,128)S(1)} %get-tuple-element.92), channel_id=1, source_target_pairs={{0,1},{1,2},{2,3},{3,4},{4,5},{5,6},{6,7},{7,8},{8,9},{9,10},{10,1... | collective-permute-start | bytes 786440 | tf_op jit(solution)/shard_map/ppermute | solution.py:14
  12.9 67.5 %copy-start.5 = (f32[1,2,256,128]{3,2,1,0:T(8,128)}, f32[1,2,256,128]{3,2,1,0:T(8,128)S(1)}, u32[]{:S(2)}) copy-start(f32[1,2,256,128]{3,2,1,0:T(8,128)S(1)} %get-tuple-element.86) | copy-start | bytes 786436
  12.9 172.1 %copy-start.3 = (f32[1,2,256,128]{3,2,1,0:T(8,128)}, f32[1,2,256,128]{3,2,1,0:T(8,128)S(1)}, u32[]{:S(2)}) copy-start(f32[1,2,256,128]{3,2,1,0:T(8,128)S(1)} %get-tuple-element.85) | copy-start | bytes 786436
  12.9 67.5 %copy-start.37 = (f32[2,32,128]{2,1,0:T(8,128)S(1)}, f32[2,32,128]{2,1,0:T(8,128)}, u32[]{:S(2)}) copy-start(f32[2,32,128]{2,1,0:T(8,128)} %param.17) | copy-start | bytes 98308
  12.9 95.9 %copy-start.38 = (f32[2,32,128]{2,1,0:T(8,128)S(1)}, f32[2,32,128]{2,1,0:T(8,128)}, u32[]{:S(2)}) copy-start(f32[2,32,128]{2,1,0:T(8,128)} %param.19) | copy-start | bytes 98308
  13.7 123.5 %copy-start.39 = (f32[2,32,128]{2,1,0:T(8,128)S(1)}, f32[2,32,128]{2,1,0:T(8,128)}, u32[]{:S(2)}) copy-start(f32[2,32,128]{2,1,0:T(8,128)} %param.18) | copy-start | bytes 98308
  13.7 151.9 %copy-start.41 = (f32[1,2]{1,0:T(1,128)S(1)}, f32[1,2]{1,0:T(1,128)}, u32[]{:S(2)}) copy-start(f32[1,2]{1,0:T(1,128)} %param.24) | copy-start | bytes 28
  13.7 168.5 %collective-permute-start = (f32[2,1,256,128]{3,2,1,0:T(8,128)}, f32[2,1,256,128]{3,2,1,0:T(8,128)}, u32[]{:S(2)}, u32[]{:S(2)}) collective-permute-start(f32[2,1,256,128]{3,2,1,0:T(8,128)} %get-tuple-element.99), channel_id=1, source_target_pairs={{1,0},{2,1},{3,2},{4,3},{5,4},{6,5},{7,6},{8,7},{9,8},{10,9},{11,1... | collective-permute-start | bytes 786440 | tf_op jit(solution)/shard_map/ppermute | solution.py:17
  18.5 163.7 %collective-permute-start.1 = (f32[2,1,256,128]{3,2,1,0:T(8,128)}, f32[2,1,256,128]{3,2,1,0:T(8,128)}, u32[]{:S(2)}, u32[]{:S(2)}) collective-permute-start(f32[2,1,256,128]{3,2,1,0:T(8,128)} %get-tuple-element.100), channel_id=1, source_target_pairs={{0,1},{1,2},{2,3},{3,4},{4,5},{5,6},{6,7},{7,8},{8,9},{9,10},{10,1... | collective-permute-start | bytes 786440 | tf_op jit(solution)/shard_map/ppermute | solution.py:14
  169.8 1.8 copy-start.40
  176.4 1.2 copy-start
  176.4 1.3 copy-start.12
  176.4 1.3 copy-start.15
  180.6 1.6 copy-start.6
  182.2 1.6 copy-start.25
  183.8 1.4 copy-start.2
  187.5 3.1 copy-start.9
  188.2 2.4 copy-start.7
  188.2 2.4 copy-start.4
  190.6 1.4 copy-start.16
  192.1 2.1 copy-start.18
  194.9 9.2 %collective-permute-start.2 = (f32[2,1,256,128]{3,2,1,0:T(8,128)}, f32[2,1,256,128]{3,2,1,0:T(8,128)}, u32[]{:S(2)}, u32[]{:S(2)}) collective-permute-start(f32[2,1,256,128]{3,2,1,0:T(8,128)} %get-tuple-element.97), channel_id=1, source_target_pairs={{1,0},{2,1},{3,2},{4,3},{5,4},{6,5},{7,6},{8,7},{9,8},{10,9},{11,1... | collective-permute-start | bytes 786440 | tf_op jit(solution)/shard_map/ppermute | solution.py:17
  196.8 11.4 %collective-permute-start.3 = (f32[2,1,256,128]{3,2,1,0:T(8,128)}, f32[2,1,256,128]{3,2,1,0:T(8,128)}, u32[]{:S(2)}, u32[]{:S(2)}) collective-permute-start(f32[2,1,256,128]{3,2,1,0:T(8,128)} %get-tuple-element.98), channel_id=1, source_target_pairs={{0,1},{1,2},{2,3},{3,4},{4,5},{5,6},{6,7},{7,8},{8,9},{9,10},{10,1... | collective-permute-start | bytes 786440 | tf_op jit(solution)/shard_map/ppermute | solution.py:14
  209.4 1.2 copy-start.24
  210.7 1.0 copy-start.22
  211.4 1.4 copy-start.26
  211.8 1.6 copy-start.8
  211.8 2.0 copy-start.10
  219.4 2.2 copy-start.20
  219.4 59.8 %copy-start.42 = (f32[1,2,256]{2,1,0:T(2,128)S(1)}, f32[1,2,256]{2,1,0:T(2,128)}, u32[]{:S(2)}) copy-start(f32[1,2,256]{2,1,0:T(2,128)} %param.27) | copy-start | bytes 6148
  219.4 59.8 %copy-start.13 = (f32[1,2,256,128]{3,2,1,0:T(8,128)S(1)}, f32[1,2,256,128]{3,2,1,0:T(8,128)}, u32[]{:S(2)}) copy-start(f32[1,2,256,128]{3,2,1,0:T(8,128)} %copy-done.11) | copy-start | bytes 786436
  281.3 2.5 copy-start.17
  281.3 2.5 copy-start.19
  281.4 2.5 copy-start.21
  281.4 2.5 copy-start.23
  286.6 1.0 copy-start.32
  286.6 1.2 copy-start.33
  286.6 1.3 copy-start.34
  287.9 1.0 copy-start.28
  287.9 1.1 copy-start.29
  287.9 1.3 copy-start.30
  (2 other events, 1.9 us)
Sparse Core Ops, SparseCore 0:
  290.3 56.7 reduce-scatter.1
where the time goes:
time: 355 us; the launch traced here: 354 us
  blocking collectives  198 us (56%)
  waiting for transfers between devices  61.2 us (17%)
  other arithmetic  51.8 us (15%)
  starting transfers between devices  16.2 us (5%)
  between operations  16 us (5%)
  local copies, waits for them, and re-layouts  10.5 us (3%)
    reduce_scatter x1, waiting for transfers between devices, shards(): lax.psum_scatter(jnp.stack(gradient), 'shot', scatter_dimension=2, tiled=...  57 us
    psum x1, blocking collectives, shards(): recorded = lax.psum(jnp.stack(traces), 'domain')  55.7 us
    all_gather x1, blocking collectives, shards(): lax.all_gather(tilt, 'shot', axis=1, tiled=True)  28.6 us
    all_gather x1, blocking collectives, shards(): lax.all_gather(azimuth, 'shot', axis=1, tiled=True)  28.6 us
    all_gather x1, blocking collectives, shards(): lax.all_gather(delta, 'shot', axis=1, tiled=True)  28.4 us
    all_gather x1, blocking collectives, shards(): lax.all_gather(velsq, 'shot', axis=1, tiled=True)  28.4 us
    all_gather x1, blocking collectives, shards(): lax.all_gather(epsilon, 'shot', axis=1, tiled=True)  28.4 us
    unnamed x33, other arithmetic  22 us
  transfers between devices with their start and end apart: 7, of which 2 were waited for; matrix products, arithmetic and copies ran while one was open for 6% of the time, Pallas kernels for 0%

commit v1 on v0

v1 whole, which is shorter than its diff:
```python
import functools

import jax
import jax.numpy as jnp
from jax import lax
from jax.experimental import pallas as pl
from jax.experimental.pallas import tpu as pltpu
from jax.sharding import PartitionSpec as P

MESH = pl.DeviceIdType.MESH
TILE = 8
PAD = 8

PEERS = ((0, 1), (1, 0), (3, 0), (1, 1), (3, 1), (2, 0), (2, 1))
MIRROR = tuple(PEERS.index(((4 - dx) % 4, dy)) for dx, dy in PEERS)

SIN = (1.0, -1 / 6, 1 / 120, -1 / 5040, 1 / 362880, -1 / 39916800, 1 / 6227020800)
COS = (1.0, -1 / 2, 1 / 24, -1 / 720, 1 / 40320, -1 / 3628800, 1 / 479001600, -1 / 87178291200)


def horner(square, series):
    total = jnp.float32(series[-1])
    for term in series[-2::-1]:
        total = total * square + jnp.float32(term)
    return total


def sin_cos(angle):
    square = angle * angle
    return angle * horner(square, SIN), horner(square, COS)


def sin_cos_wide(angle):
    half_sin, half_cos = sin_cos(0.5 * angle)
    return 2.0 * half_sin * half_cos, 1.0 - 2.0 * half_sin * half_sin


def hessian(pad_ref, row, first, last):
    here = pad_ref[:, pl.ds(row, TILE), :]
    above = pad_ref[:, pl.ds(row + 1, TILE), :]
    below = pad_ref[:, pl.ds(row - 1, TILE), :]

    def ahead(values):
        return jnp.where(last, 0.0, pltpu.roll(values, values.shape[-1] - 1, 2))

    def behind(values):
        return jnp.where(first, 0.0, pltpu.roll(values, 1, 2))

    center = here[1:3]
    twice = 2.0 * center
    along_x = here[2:4] - here[0:2]
    along_y = above[1:3] - below[1:3]
    xx = here[2:4] + here[0:2] - twice
    yy = above[1:3] + below[1:3] - twice
    zz = ahead(center) + behind(center) - twice
    xy = (above[2:4] - above[0:2]) - (below[2:4] - below[0:2])
    xz = ahead(along_x) - behind(along_x)
    yz = ahead(along_y) - behind(along_y)
    return center, (xx, yy, zz, xy, xz, yz)


def times_axis(parts, axis, quarter):
    xx, yy, zz, xy, xz, yz = parts
    return (
        xx * axis[0] + xy * quarter[1] + xz * quarter[2],
        xy * quarter[0] + yy * axis[1] + yz * quarter[2],
        xz * quarter[0] + yz * quarter[1] + zz * axis[2],
    )


def dot3(left, right):
    return left[0] * right[0] + left[1] * right[1] + left[2] * right[2]


def kernel(
    velsq,
    epsilon,
    delta,
    tilt,
    azimuth,
    forward,
    adjoint,
    wavelet,
    source,
    receivers,
    observed,
    out,
    coef,
    pad_p,
    pad_q,
    pad_a,
    pad_b,
    pad_p1,
    pad_q1,
    olds,
    table,
    terms,
    step_a,
    hits,
    grad,
    parts,
    local_sem,
    gather_send,
    gather_recv,
    halo_send,
    halo_recv,
    next_send,
    next_recv,
    sum_send,
    sum_recv,
):
    shot = lax.axis_index("shot")
    domain = lax.axis_index("domain")
    slabs = lax.axis_size("domain")
    rows = pad_p.shape[1] - 2 * PAD
    block = coef.shape[3]
    blocks = coef.shape[0]
    lanes = pad_p.shape[2]
    has_low = domain > 0
    has_high = domain < slabs - 1

    def other(dx, dy):
        return lax.rem(shot // 2 + dx, 4) * 2 + lax.rem(lax.rem(shot, 2) + dy, 2)

    def step_of(place):
        dx = jnp.where(
            (place == 2) | (place == 4), 1, jnp.where((place == 3) | (place == 5), 3, jnp.where(place >= 6, 2, 0))
        )
        dy = jnp.where((place == 1) | (place == 4) | (place == 5) | (place == 7), 1, 0)
        return other(dx, dy)

    locals_ = []

    def local(src, dst):
        copy = pltpu.make_async_copy(src, dst, local_sem.at[len(locals_)])
        copy.start()
        locals_.append(copy)

    for place, field in enumerate((velsq, epsilon, delta, tilt, azimuth)):
        local(field, coef.at[shot, place])
    inside = pl.ds(PAD, rows)
    for pad, state, place in ((pad_p, forward, 1), (pad_q, forward, 3), (pad_a, adjoint, 1), (pad_b, adjoint, 3)):
        local(state.at[0, place], pad.at[pl.ds(1, 2), inside])
    for place, (state, member) in enumerate(((forward, 0), (forward, 2), (adjoint, 0), (adjoint, 2))):
        local(state.at[0, member], olds.at[place])

    barrier = pltpu.get_barrier_semaphore()
    for dx, dy in PEERS:
        pl.semaphore_signal(barrier, inc=1, device_id=(other(dx, dy), domain), device_id_type=MESH)

    @pl.when(has_low)
    def _():
        pl.semaphore_signal(barrier, inc=1, device_id=(shot, domain - 1), device_id_type=MESH)

    @pl.when(has_high)
    def _():
        pl.semaphore_signal(barrier, inc=1, device_id=(shot, domain + 1), device_id_type=MESH)

    for pad in (pad_p, pad_q, pad_a, pad_b, pad_p1, pad_q1):
        zero = jnp.zeros((4, PAD, lanes), jnp.float32)
        pad[:, 0:PAD, :] = zero
        pad[:, PAD + rows : 2 * PAD + rows, :] = zero

    @pl.when(jnp.logical_not(has_low))
    def _():
        for pad in (pad_p, pad_q, pad_a, pad_b, pad_p1, pad_q1):
            pad[0, PAD : PAD + rows, :] = jnp.zeros((rows, lanes), jnp.float32)

    @pl.when(jnp.logical_not(has_high))
    def _():
        for pad in (pad_p, pad_q, pad_a, pad_b, pad_p1, pad_q1):
            pad[3, PAD : PAD + rows, :] = jnp.zeros((rows, lanes), jnp.float32)

    pl.semaphore_wait(barrier, len(PEERS) + has_low.astype(jnp.int32) + has_high.astype(jnp.int32))

    def halo(src_low, src_high, pad, span, sems_send, sems_recv, low, high):
        down = pltpu.make_async_remote_copy(
            src_ref=src_low,
            dst_ref=pad.at[3, span],
            send_sem=sems_send.at[low],
            recv_sem=sems_recv.at[low],
            device_id=(shot, domain - 1),
            device_id_type=MESH,
        )
        up = pltpu.make_async_remote_copy(
            src_ref=src_high,
            dst_ref=pad.at[0, span],
            send_sem=sems_send.at[high],
            recv_sem=sems_recv.at[high],
            device_id=(shot, domain + 1),
            device_id_type=MESH,
        )
        return down, up

    def begin(pair):
        pl.when(has_low)(pair[0].start)
        pl.when(has_high)(pair[1].start)

    def arrived(pair):
        pl.when(has_high)(pair[0].wait_recv)
        pl.when(has_low)(pair[1].wait_recv)

    def sent(pair):
        pl.when(has_low)(pair[0].wait_send)
        pl.when(has_high)(pair[1].wait_send)

    first_halo = []
    for place, (pad, state, member) in enumerate(
        ((pad_p, forward, 1), (pad_q, forward, 3), (pad_a, adjoint, 1), (pad_b, adjoint, 3))
    ):
        first_halo.append(
            halo(state.at[0, member, 0], state.at[0, member, 1], pad, inside, halo_send, halo_recv, 2 * place, 2 * place + 1)
        )
    begin(first_halo[0])
    begin(first_halo[1])

    for copy in locals_[0:5]:
        copy.wait()

    def gather(place, dx, dy):
        return pltpu.make_async_remote_copy(
            src_ref=coef.at[shot],
            dst_ref=coef.at[shot],
            send_sem=gather_send.at[place],
            recv_sem=gather_recv.at[MIRROR[place]],
            device_id=(other(dx, dy), domain),
            device_id_type=MESH,
        )

    gathers = [gather(place, dx, dy) for place, (dx, dy) in enumerate(PEERS)]
    for copy in gathers:
        copy.start()
    begin(first_halo[2])
    begin(first_halo[3])

    cells = receivers[...] - domain * (2 * rows * lanes)
    at_row = lax.shift_right_arithmetic(cells, 7)
    at_lane = cells & (lanes - 1)
    count = cells.shape[1]
    lane_of = lax.broadcasted_iota(jnp.int32, (lanes, count), 0)
    by_lane = jnp.where(lane_of == at_lane, 1.0, 0.0)
    recorded = by_lane * observed[0, 1:2, :]
    contract = (((1,), (1,)), ((), ()))
    for plane in range(2):
        row_of = lax.broadcasted_iota(jnp.int32, (rows, count), 0) + plane * rows
        by_row = jnp.where(row_of == at_row, 1.0, 0.0)
        hits[0, plane] = lax.dot_general(
            by_row, by_lane, contract, precision=lax.Precision.HIGHEST, preferred_element_type=jnp.float32
        )
        hits[1, plane] = lax.dot_general(
            by_row, recorded, contract, precision=lax.Precision.HIGHEST, preferred_element_type=jnp.float32
        )

    shape = (2, TILE, lanes)
    lane = lax.broadcasted_iota(jnp.int32, shape, 2)
    first = lane == 0
    last = lane == lanes - 1
    cell = lax.broadcasted_iota(jnp.int32, shape, 0) * (rows * lanes) + lax.broadcasted_iota(jnp.int32, shape, 1) * lanes + lane
    source_at = source[0] - domain * (2 * rows * lanes)

    def at_source(row, amount):
        return jnp.where(cell == source_at - row * lanes, amount, 0.0)

    for copy in locals_[5:]:
        copy.wait()
    arrived(first_halo[0])
    arrived(first_halo[1])

    def next_halo(owner):
        span = pl.ds(pl.multiple_of(owner * block + PAD, TILE), block)
        pairs = []
        for place, pad in enumerate((pad_p1, pad_q1)):
            at = (owner * 2 + place) * 2
            pairs.append(halo(pad.at[1, span], pad.at[2, span], pad, span, next_send, next_recv, at, at + 1))
        return pairs

    def forward_tile(owner, tile):
        inner = pl.ds(pl.multiple_of(tile * TILE, TILE), TILE)
        row = pl.multiple_of(owner * block + tile * TILE, TILE)
        span = pl.ds(row, TILE)
        speed, eps, dlt, til, azi = (coef[owner, place, :, inner, :] for place in range(5))
        sin_t, cos_t = sin_cos(til)
        sin_a, cos_a = sin_cos_wide(azi)
        axis = (sin_t * cos_a, sin_t * sin_a, cos_t)
        turn = (cos_t * cos_a, cos_t * sin_a, -sin_t)
        quarter = tuple(0.25 * part for part in axis)
        stretch = 1.0 + 2.0 * eps
        root = jnp.sqrt(1.0 + 2.0 * dlt)
        for place, values in enumerate(axis + turn + (stretch, root, speed)):
            table[place, :, span, :] = values
        here_p, hess_p = hessian(pad_p, row + PAD, first, last)
        here_q, hess_q = hessian(pad_q, row + PAD, first, last)
        lean_p = times_axis(hess_p, axis, quarter)
        lean_q = times_axis(hess_q, axis, quarter)
        across = hess_p[0] + hess_p[1] + hess_p[2] - dot3(axis, lean_p)
        axial = dot3(axis, lean_q)
        drive_p = stretch * across + root * axial
        drive_q = root * across + axial
        pulse = at_source(row, wavelet[0, 0])
        here = pl.ds(pl.multiple_of(row + PAD, TILE), TILE)
        pad_p1[1:3, here, :] = 2.0 * here_p - olds[0, :, span, :] + speed * drive_p + pulse
        pad_q1[1:3, here, :] = 2.0 * here_q - olds[1, :, span, :] + speed * drive_q + pulse
        for place, values in enumerate(
            (
                across,
                axial,
                2.0 * dot3(turn, lean_p),
                2.0 * dot3(turn, lean_q),
                2.0 * (axis[0] * lean_p[1] - axis[1] * lean_p[0]),
                2.0 * (axis[0] * lean_q[1] - axis[1] * lean_q[0]),
            )
        ):
            terms[place, :, span, :] = values

    tiles = block // TILE

    def forward_block(place, carry):
        owner = step_of(place)

        @pl.when(place > 0)
        def _():
            pltpu.make_async_copy(coef.at[owner], coef.at[owner], gather_recv.at[place - 1]).wait()

        lax.fori_loop(0, tiles, lambda tile, c: (forward_tile(owner, tile), c)[1], 0)
        for pair in next_halo(owner):
            begin(pair)
        return carry

    lax.fori_loop(0, blocks, forward_block, 0)

    arrived(first_halo[2])
    arrived(first_halo[3])

    def load_table(span):
        values = tuple(table[place, :, span, :] for place in range(9))
        return values[0:3], values[3:6], values[6], values[7], values[8]

    def adjoint_tile(tile, carry):
        row = pl.multiple_of(tile * TILE, TILE)
        span = pl.ds(row, TILE)
        axis, _, stretch, root, speed = load_table(span)
        quarter = tuple(0.25 * part for part in axis)
        here_a, hess_a = hessian(pad_a, row + PAD, first, last)
        here_b, hess_b = hessian(pad_b, row + PAD, first, last)
        across = hess_a[0] + hess_a[1] + hess_a[2] - dot3(axis, times_axis(hess_a, axis, quarter))
        axial = dot3(axis, times_axis(hess_b, axis, quarter))
        step_a[0, :, span, :] = 2.0 * here_a - olds[2, :, span, :] + speed * (stretch * across + root * axial)
        step_a[1, :, span, :] = 2.0 * here_b - olds[3, :, span, :] + speed * (root * across + axial)
        return carry

    lax.fori_loop(0, rows // TILE, adjoint_tile, 0)

    def halo_in(owner, carry):
        for pair in next_halo(owner):
            arrived(pair)
        return carry

    lax.fori_loop(0, blocks, halo_in, 0)

    def gradient_tile(owner, tile):
        inner = pl.ds(pl.multiple_of(tile * TILE, TILE), TILE)
        row = pl.multiple_of(owner * block + tile * TILE, TILE)
        span = pl.ds(row, TILE)
        axis, turn, stretch, root, speed = load_table(span)
        quarter = tuple(0.25 * part for part in axis)
        here_p, hess_p = hessian(pad_p1, row + PAD, first, last)
        _, hess_q = hessian(pad_q1, row + PAD, first, last)
        lean_p = times_axis(hess_p, axis, quarter)
        lean_q = times_axis(hess_q, axis, quarter)
        across1 = hess_p[0] + hess_p[1] + hess_p[2] - dot3(axis, lean_p)
        axial1 = dot3(axis, lean_q)
        here = pl.ds(pl.multiple_of(row + PAD, TILE), TILE)
        last_p = 2.0 * here_p - pad_p[1:3, here, :] + speed * (stretch * across1 + root * axial1)
        last_p = last_p + at_source(row, wavelet[0, 1])
        late_a, late_b = pad_a[1:3, here, :], pad_b[1:3, here, :]
        early_a = step_a[0, :, span, :] + (hits[0, :, span, :] * last_p - hits[1, :, span, :])
        early_b = step_a[1, :, span, :]
        across0, axial0, tilt_p0, tilt_q0, spin_p0, spin_q0 = (terms[place, :, span, :] for place in range(6))
        tilt_p1 = 2.0 * dot3(turn, lean_p)
        tilt_q1 = 2.0 * dot3(turn, lean_q)
        spin_p1 = 2.0 * (axis[0] * lean_p[1] - axis[1] * lean_p[0])
        spin_q1 = 2.0 * (axis[0] * lean_q[1] - axis[1] * lean_q[0])
        by_stretch = early_a * across0 + late_a * across1
        by_root = early_a * axial0 + early_b * across0 + late_a * axial1 + late_b * across1
        by_one = early_b * axial0 + late_b * axial1

        def turned(p0, q0, p1, q1):
            return speed * (
                root * (early_a * q0 - early_b * p0 + late_a * q1 - late_b * p1)
                - stretch * (early_a * p0 + late_a * p1)
                + (early_b * q0 + late_b * q1)
            )

        for place, values in enumerate(
            (
                stretch * by_stretch + root * by_root + by_one,
                2.0 * speed * by_stretch,
                speed * by_root / root,
                turned(tilt_p0, tilt_q0, tilt_p1, tilt_q1),
                turned(spin_p0, spin_q0, spin_p1, spin_q1),
            )
        ):
            grad[owner, place, :, inner, :] = values

    def summand(place, owner):
        mirror = jnp.where(
            (place == 1) | (place == 3), place + 1, jnp.where((place == 2) | (place == 4), place - 1, place)
        )
        return pltpu.make_async_remote_copy(
            src_ref=grad.at[owner],
            dst_ref=parts.at[mirror],
            send_sem=sum_send.at[place],
            recv_sem=sum_recv.at[mirror],
            device_id=(owner, domain),
            device_id_type=MESH,
        )

    def gradient_block(turn_at, carry):
        place = blocks - 1 - turn_at
        owner = step_of(place)
        lax.fori_loop(0, tiles, lambda tile, c: (gradient_tile(owner, tile), c)[1], 0)

        @pl.when(place > 0)
        def _():
            summand(place - 1, owner).start()

        return carry

    lax.fori_loop(0, blocks, gradient_block, 0)

    def add_part(place, carry):
        summand(place, step_of(place + 1)).wait_recv()
        return carry

    lax.fori_loop(0, blocks - 1, add_part, 0)
    total = grad[shot]
    for place in range(blocks - 1):
        total = total + parts[place]
    out[...] = total

    for copy in gathers:
        copy.wait_send()
    for pair in first_halo:
        sent(pair)

    def drained(owner, carry):
        for pair in next_halo(owner):
            sent(pair)
        return carry

    lax.fori_loop(0, blocks, drained, 0)

    def parts_left(place, carry):
        summand(place, step_of(place + 1)).wait_send()
        return carry

    lax.fori_loop(0, blocks - 1, parts_left, 0)


def shards(velsq, epsilon, delta, tilt, azimuth, forward, adjoint, wavelet, source, receivers, observed):
    planes, block, lanes = velsq.shape
    rows = forward.shape[3]
    blocks = rows // block
    padded = pltpu.VMEM((planes + 2, rows + 2 * PAD, lanes), jnp.float32)
    anywhere = pl.BlockSpec(memory_space=pl.ANY)
    vmem = pl.BlockSpec(memory_space=pltpu.VMEM)
    smem = pl.BlockSpec(memory_space=pltpu.SMEM)

    def fields(*lead):
        return pltpu.VMEM(lead + (planes, rows, lanes), jnp.float32)

    def by_block(count):
        return pltpu.VMEM((count, 5, planes, block, lanes), jnp.float32)

    sems = pltpu.SemaphoreType.DMA
    return pl.pallas_call(
        kernel,
        out_shape=jax.ShapeDtypeStruct((5, planes, block, lanes), jnp.float32),
        in_specs=[anywhere] * 7 + [smem, smem, vmem, vmem],
        out_specs=vmem,
        scratch_shapes=[by_block(blocks)]
        + [padded] * 6
        + [fields(4), fields(9), fields(6), fields(2), fields(2), by_block(blocks), by_block(blocks - 1)]
        + [
            sems((13,)),
            sems((blocks - 1,)),
            sems((blocks - 1,)),
            sems((8,)),
            sems((8,)),
            sems((4 * blocks,)),
            sems((4 * blocks,)),
            sems((blocks - 1,)),
            sems((blocks - 1,)),
        ],
        compiler_params=pltpu.CompilerParams(
            collective_id=0, has_side_effects=True, vmem_limit_bytes=40 << 20
        ),
        name="gradient",
    )(velsq, epsilon, delta, tilt, azimuth, forward, adjoint, wavelet, source, receivers, observed)


def solution(mesh):
    field = P("domain", "shot", None)
    state = P("shot", None, "domain", None, None)
    return jax.shard_map(
        shards,
        mesh=mesh,
        in_specs=(field,) * 5 + (state, state, P("shot", None), P("shot"), P("shot", None), P("shot", None, None)),
        out_specs=P(None, "domain", "shot", None),
        check_vma=False,
    )
```

time: 355 us -> 65.3 us (0.18)
  the two profiles are of different devices: /device:TPU:48 before, /device:TPU:193 now
where the time goes in v1:
time: 65.3 us; the launch traced here: 64.8 us
  Pallas kernels  56.5 us (87%)
  local copies, waits for them, and re-layouts  7.59 us (12%)
  between operations  0.72 us (1%)
    pallas_call x1, Pallas kernels, shards(): pl.pallas_call(kernel, out_shape=jax.ShapeDtypeStruct((5, planes, block,...  56.5 us
    unnamed x21, local copies, waits for them, and re-layouts  7.59 us

profile of v1, /device:TPU:193, one launch (start us, length us, event | category | flops | bytes accessed | tf_op | source)
XLA Modules:
  0.0 64.8 jit_solution(11574368250043089888)
XLA Ops:
  0.0 0.0 copy-start.8
  0.0 0.0 copy-start.9
  0.7 0.0 copy-done.8
  0.7 0.0 copy-done.9
  0.7 0.0 copy-start
  0.7 1.2 %copy-done = f32[1,4,2,256,128]{4,3,2,1,0:T(8,128)S(1)} copy-done((f32[1,4,2,256,128]{4,3,2,1,0:T(8,128)S(1)}, f32[1,4,2,256,128]{4,3,2,1,0:T(8,128)}, u32[]{:S(2)}) %copy-start) | copy-done | bytes 1048600
  1.9 0.0 copy-start.1
  1.9 1.2 %copy-done.1 = f32[1,4,2,256,128]{4,3,2,1,0:T(8,128)S(1)} copy-done((f32[1,4,2,256,128]{4,3,2,1,0:T(8,128)S(1)}, f32[1,4,2,256,128]{4,3,2,1,0:T(8,128)}, u32[]{:S(2)}) %copy-start.1) | copy-done | bytes 1048600
  3.2 0.0 copy-start.2
  3.2 0.8 %copy-done.2 = f32[2,32,128]{2,1,0:T(8,128)S(1)} copy-done((f32[2,32,128]{2,1,0:T(8,128)S(1)}, f32[2,32,128]{2,1,0:T(8,128)}, u32[]{:S(2)}) %copy-start.2) | copy-done | bytes 32792
  3.9 0.0 copy-start.3
  3.9 0.8 %copy-done.3 = f32[2,32,128]{2,1,0:T(8,128)S(1)} copy-done((f32[2,32,128]{2,1,0:T(8,128)S(1)}, f32[2,32,128]{2,1,0:T(8,128)}, u32[]{:S(2)}) %copy-start.3) | copy-done | bytes 32792
  4.7 0.0 copy-start.4
  4.7 0.8 %copy-done.4 = f32[2,32,128]{2,1,0:T(8,128)S(1)} copy-done((f32[2,32,128]{2,1,0:T(8,128)S(1)}, f32[2,32,128]{2,1,0:T(8,128)}, u32[]{:S(2)}) %copy-start.4) | copy-done | bytes 32792
  5.4 0.0 copy-start.5
  5.4 0.8 %copy-done.5 = f32[2,32,128]{2,1,0:T(8,128)S(1)} copy-done((f32[2,32,128]{2,1,0:T(8,128)S(1)}, f32[2,32,128]{2,1,0:T(8,128)}, u32[]{:S(2)}) %copy-start.5) | copy-done | bytes 32792
  6.2 0.0 copy-start.6
  6.2 0.8 %copy-done.6 = f32[2,32,128]{2,1,0:T(8,128)S(1)} copy-done((f32[2,32,128]{2,1,0:T(8,128)S(1)}, f32[2,32,128]{2,1,0:T(8,128)}, u32[]{:S(2)}) %copy-start.6) | copy-done | bytes 32792
  6.9 0.0 copy-start.7
  6.9 0.7 %copy-done.7 = f32[1,2,256]{2,1,0:T(2,128)S(1)} copy-done((f32[1,2,256]{2,1,0:T(2,128)S(1)}, f32[1,2,256]{2,1,0:T(2,128)}, u32[]{:S(2)}) %copy-start.7) | copy-done | bytes 2072
  7.6 56.5 %gradient.1 = f32[5,2,32,128]{3,2,1,0:T(8,128)S(1)} custom-call(f32[2,32,128]{2,1,0:T(8,128)S(1)} %copy-done.2, f32[2,32,128]{2,1,0:T(8,128)S(1)} %copy-done.3, f32[2,32,128]{2,1,0:T(8,128)S(1)} %copy-done.4, f32[2,32,128]{2,1,0:T(8,128)S(1)} %copy-done.5, f32[2,32,128]{2,1,0:T(8,128)S(1)} %copy-done.6, f32[1,4,2,256,128]{4,3,2,1,0:T(8,128)S(1)} %copy-done, ...), custom_call_target="tpu_custom_call" | custom-call | tf_op jit(solution)/shard_map/gradient/pallas_call | solution.py:476
  64.1 0.7 %copy.14 = f32[5,2,32,128]{3,2,1,0:T(8,128)} copy(f32[5,2,32,128]{3,2,1,0:T(8,128)S(1)} %gradient.1) | data formatting | bytes 327680
Async XLA Ops:
  0.0 0.7 %copy-start.8 = (s32[1,256]{1,0:T(1,128)S(1)}, s32[1,256]{1,0:T(1,128)}, u32[]{:S(2)}) copy-start(s32[1,256]{1,0:T(1,128)} %receivers.1) | copy-start | bytes 3076
  0.0 0.7 %copy-start.9 = (f32[1,2]{1,0:T(1,128)S(1)}, f32[1,2]{1,0:T(1,128)}, u32[]{:S(2)}) copy-start(f32[1,2]{1,0:T(1,128)} %wavelet.1) | copy-start | bytes 28
  0.7 1.2 %copy-start = (f32[1,4,2,256,128]{4,3,2,1,0:T(8,128)S(1)}, f32[1,4,2,256,128]{4,3,2,1,0:T(8,128)}, u32[]{:S(2)}) copy-start(f32[1,4,2,256,128]{4,3,2,1,0:T(8,128)} %forward.1) | copy-start | bytes 3145732
  1.9 1.2 %copy-start.1 = (f32[1,4,2,256,128]{4,3,2,1,0:T(8,128)S(1)}, f32[1,4,2,256,128]{4,3,2,1,0:T(8,128)}, u32[]{:S(2)}) copy-start(f32[1,4,2,256,128]{4,3,2,1,0:T(8,128)} %adjoint.1) | copy-start | bytes 3145732
  3.2 0.8 %copy-start.2 = (f32[2,32,128]{2,1,0:T(8,128)S(1)}, f32[2,32,128]{2,1,0:T(8,128)}, u32[]{:S(2)}) copy-start(f32[2,32,128]{2,1,0:T(8,128)} %velsq.1) | copy-start | bytes 98308
  3.9 0.8 %copy-start.3 = (f32[2,32,128]{2,1,0:T(8,128)S(1)}, f32[2,32,128]{2,1,0:T(8,128)}, u32[]{:S(2)}) copy-start(f32[2,32,128]{2,1,0:T(8,128)} %epsilon.1) | copy-start | bytes 98308
  4.7 0.8 %copy-start.4 = (f32[2,32,128]{2,1,0:T(8,128)S(1)}, f32[2,32,128]{2,1,0:T(8,128)}, u32[]{:S(2)}) copy-start(f32[2,32,128]{2,1,0:T(8,128)} %delta.1) | copy-start | bytes 98308
  5.4 0.8 %copy-start.5 = (f32[2,32,128]{2,1,0:T(8,128)S(1)}, f32[2,32,128]{2,1,0:T(8,128)}, u32[]{:S(2)}) copy-start(f32[2,32,128]{2,1,0:T(8,128)} %tilt.1) | copy-start | bytes 98308
  6.2 0.8 %copy-start.6 = (f32[2,32,128]{2,1,0:T(8,128)S(1)}, f32[2,32,128]{2,1,0:T(8,128)}, u32[]{:S(2)}) copy-start(f32[2,32,128]{2,1,0:T(8,128)} %azimuth.1) | copy-start | bytes 98308
  6.9 0.7 %copy-start.7 = (f32[1,2,256]{2,1,0:T(2,128)S(1)}, f32[1,2,256]{2,1,0:T(2,128)}, u32[]{:S(2)}) copy-start(f32[1,2,256]{2,1,0:T(2,128)} %observed.1) | copy-start | bytes 6148

commit v2 on v1

--- a/solution.py
+++ b/solution.py
@@ -11,8 +11,6 @@
 TILE = 8
 PAD = 8
 
-PEERS = ((0, 1), (1, 0), (3, 0), (1, 1), (3, 1), (2, 0), (2, 1))
-MIRROR = tuple(PEERS.index(((4 - dx) % 4, dy)) for dx, dy in PEERS)
 
 SIN = (1.0, -1 / 6, 1 / 120, -1 / 5040, 1 / 362880, -1 / 39916800, 1 / 6227020800)
 COS = (1.0, -1 / 2, 1 / 24, -1 / 720, 1 / 40320, -1 / 3628800, 1 / 479001600, -1 / 87178291200)
@@ -98,7 +96,9 @@
     step_a,
     hits,
     grad,
-    parts,
+    far,
+    near,
+    mates,
     local_sem,
     gather_send,
     gather_recv,
@@ -106,8 +106,12 @@
     halo_recv,
     next_send,
     next_recv,
-    sum_send,
-    sum_recv,
+    far_send,
+    far_recv,
+    near_send,
+    near_recv,
+    mate_send,
+    mate_recv,
 ):
     shot = lax.axis_index("shot")
     domain = lax.axis_index("domain")
@@ -137,7 +141,7 @@
         locals_.append(copy)
 
     for place, field in enumerate((velsq, epsilon, delta, tilt, azimuth)):
-        local(field, coef.at[shot, place])
+        local(field, coef.at[shot, :, place])
     inside = pl.ds(PAD, rows)
     for pad, state, place in ((pad_p, forward, 1), (pad_q, forward, 3), (pad_a, adjoint, 1), (pad_b, adjoint, 3)):
         local(state.at[0, place], pad.at[pl.ds(1, 2), inside])
@@ -145,8 +149,9 @@
         local(state.at[0, member], olds.at[place])
 
     barrier = pltpu.get_barrier_semaphore()
-    for dx, dy in PEERS:
-        pl.semaphore_signal(barrier, inc=1, device_id=(other(dx, dy), domain), device_id_type=MESH)
+    mate, right, left = other(0, 1), other(1, 0), other(3, 0)
+    for peer in (mate, right, left):
+        pl.semaphore_signal(barrier, inc=1, device_id=(peer, domain), device_id_type=MESH)
 
     @pl.when(has_low)
     def _():
@@ -171,7 +176,7 @@
         for pad in (pad_p, pad_q, pad_a, pad_b, pad_p1, pad_q1):
             pad[3, PAD : PAD + rows, :] = jnp.zeros((rows, lanes), jnp.float32)
 
-    pl.semaphore_wait(barrier, len(PEERS) + has_low.astype(jnp.int32) + has_high.astype(jnp.int32))
+    pl.semaphore_wait(barrier, 3 + has_low.astype(jnp.int32) + has_high.astype(jnp.int32))
 
     def halo(src_low, src_high, pad, span, sems_send, sems_recv, low, high):
         down = pltpu.make_async_remote_copy(
@@ -211,27 +216,36 @@
         first_halo.append(
             halo(state.at[0, member, 0], state.at[0, member, 1], pad, inside, halo_send, halo_recv, 2 * place, 2 * place + 1)
         )
+    def push(part, peer, send_sem, recv_sem):
+        return pltpu.make_async_remote_copy(
+            src_ref=part,
+            dst_ref=part,
+            send_sem=send_sem,
+            recv_sem=recv_sem,
+            device_id=(peer, domain),
+            device_id_type=MESH,
+        )
+
+    def landed(part, recv_sem):
+        pltpu.make_async_copy(part, part, recv_sem).wait()
+
+    sends = [
+        push(coef.at[shot], mate, gather_send.at[0], gather_recv.at[1]),
+        push(coef.at[shot], right, gather_send.at[1], gather_recv.at[3]),
+        push(coef.at[shot], left, gather_send.at[2], gather_recv.at[2]),
+        push(coef.at[mate], right, gather_send.at[3], gather_recv.at[5]),
+        push(coef.at[mate], left, gather_send.at[4], gather_recv.at[4]),
+        push(coef.at[left, 0], right, gather_send.at[5], gather_recv.at[6]),
+        push(coef.at[right, 1], left, gather_send.at[6], gather_recv.at[7]),
+        push(coef.at[other(3, 1), 0], right, gather_send.at[7], gather_recv.at[8]),
+        push(coef.at[other(1, 1), 1], left, gather_send.at[8], gather_recv.at[9]),
+    ]
+    for copy in locals_[0:5]:
+        copy.wait()
+    for copy in sends[0:3]:
+        copy.start()
     begin(first_halo[0])
     begin(first_halo[1])
-
-    for copy in locals_[0:5]:
-        copy.wait()
-
-    def gather(place, dx, dy):
-        return pltpu.make_async_remote_copy(
-            src_ref=coef.at[shot],
-            dst_ref=coef.at[shot],
-            send_sem=gather_send.at[place],
-            recv_sem=gather_recv.at[MIRROR[place]],
-            device_id=(other(dx, dy), domain),
-            device_id_type=MESH,
-        )
-
-    gathers = [gather(place, dx, dy) for place, (dx, dy) in enumerate(PEERS)]
-    for copy in gathers:
-        copy.start()
-    begin(first_halo[2])
-    begin(first_halo[3])
 
     cells = receivers[...] - domain * (2 * rows * lanes)
     at_row = lax.shift_right_arithmetic(cells, 7)
@@ -261,6 +275,15 @@
     def at_source(row, amount):
         return jnp.where(cell == source_at - row * lanes, amount, 0.0)
 
+    landed(coef.at[mate], gather_recv.at[1])
+    sends[3].start()
+    sends[4].start()
+    landed(coef.at[left], gather_recv.at[3])
+    sends[5].start()
+    landed(coef.at[right], gather_recv.at[2])
+    sends[6].start()
+    begin(first_halo[2])
+    begin(first_halo[3])
     for copy in locals_[5:]:
         copy.wait()
     arrived(first_halo[0])
@@ -278,7 +301,7 @@
         inner = pl.ds(pl.multiple_of(tile * TILE, TILE), TILE)
         row = pl.multiple_of(owner * block + tile * TILE, TILE)
         span = pl.ds(row, TILE)
-        speed, eps, dlt, til, azi = (coef[owner, place, :, inner, :] for place in range(5))
+        speed, eps, dlt, til, azi = (coef[owner, :, place, inner, :] for place in range(5))
         sin_t, cos_t = sin_cos(til)
         sin_a, cos_a = sin_cos_wide(azi)
         axis = (sin_t * cos_a, sin_t * sin_a, cos_t)
@@ -317,9 +340,17 @@
     def forward_block(place, carry):
         owner = step_of(place)
 
-        @pl.when(place > 0)
+        @pl.when(place == 3)
         def _():
-            pltpu.make_async_copy(coef.at[owner], coef.at[owner], gather_recv.at[place - 1]).wait()
+            landed(coef.at[other(3, 1)], gather_recv.at[5])
+            sends[7].start()
+            landed(coef.at[other(1, 1)], gather_recv.at[4])
+            sends[8].start()
+
+        @pl.when(place >= 6)
+        def _():
+            for plane in range(2):
+                landed(coef.at[owner, plane], gather_recv.at[2 * place - 6 + plane])
 
         lax.fori_loop(0, tiles, lambda tile, c: (forward_tile(owner, tile), c)[1], 0)
         for pair in next_halo(owner):
@@ -400,45 +431,79 @@
                 turned(spin_p0, spin_q0, spin_p1, spin_q1),
             )
         ):
-            grad[owner, place, :, inner, :] = values
-
-    def summand(place, owner):
-        mirror = jnp.where(
-            (place == 1) | (place == 3), place + 1, jnp.where((place == 2) | (place == 4), place - 1, place)
-        )
+            grad[owner, :, place, inner, :] = values
+
+    def far_part(side, where):
         return pltpu.make_async_remote_copy(
-            src_ref=grad.at[owner],
-            dst_ref=parts.at[mirror],
-            send_sem=sum_send.at[place],
-            recv_sem=sum_recv.at[mirror],
-            device_id=(owner, domain),
+            src_ref=grad.at[other(2, where), side],
+            dst_ref=far.at[side, where],
+            send_sem=far_send.at[2 * side + where],
+            recv_sem=far_recv.at[2 * side + where],
+            device_id=((right, left)[side], domain),
             device_id_type=MESH,
         )
 
+    def near_part(side, where):
+        return pltpu.make_async_remote_copy(
+            src_ref=grad.at[other((1, 3)[side], where)],
+            dst_ref=near.at[side, where],
+            send_sem=near_send.at[2 * side + where],
+            recv_sem=near_recv.at[2 * side + where],
+            device_id=((right, left)[side], domain),
+            device_id_type=MESH,
+        )
+
+    def pass_sums(where):
+        for side in range(2):
+            owner = other((1, 3)[side], where)
+            far_part(side, where).wait_recv()
+            grad[owner, side] = grad[owner, side] + far[side, where]
+            near_part(side, where).start()
+
     def gradient_block(turn_at, carry):
-        place = blocks - 1 - turn_at
+        place = jnp.where(
+            turn_at < 2,
+            7 - turn_at,
+            jnp.where(turn_at < 4, turn_at + 2, jnp.where(turn_at < 6, turn_at - 2, 7 - turn_at)),
+        )
         owner = step_of(place)
         lax.fori_loop(0, tiles, lambda tile, c: (gradient_tile(owner, tile), c)[1], 0)
-
-        @pl.when(place > 0)
-        def _():
-            summand(place - 1, owner).start()
+        for where in range(2):
+
+            @pl.when(turn_at == 1 - where)
+            def _():
+                for side in range(2):
+                    far_part(side, where).start()
+
+            @pl.when(turn_at == 5 - 2 * where)
+            def _():
+                pass_sums(where)
 
         return carry
 
     lax.fori_loop(0, blocks, gradient_block, 0)
 
-    def add_part(place, carry):
-        summand(place, step_of(place + 1)).wait_recv()
-        return carry
-
-    lax.fori_loop(0, blocks - 1, add_part, 0)
-    total = grad[shot]
-    for place in range(blocks - 1):
-        total = total + parts[place]
-    out[...] = total
-
-    for copy in gathers:
+    swap = pltpu.make_async_remote_copy(
+        src_ref=grad.at[mate],
+        dst_ref=mates,
+        send_sem=mate_send,
+        recv_sem=mate_recv,
+        device_id=(mate, domain),
+        device_id_type=MESH,
+    )
+    for side in range(2):
+        near_part(side, 1).wait_recv()
+    grad[mate] = grad[mate] + (near[0, 1] + near[1, 1])
+    swap.start()
+    for side in range(2):
+        near_part(side, 0).wait_recv()
+    total = grad[shot] + (near[0, 0] + near[1, 0])
+    swap.wait_recv()
+    total = total + mates[...]
+    for plane in range(2):
+        out[:, plane] = total[plane]
+
+    for copy in sends:
         copy.wait_send()
     for pair in first_halo:
         sent(pair)
@@ -449,12 +514,11 @@
         return carry
 
     lax.fori_loop(0, blocks, drained, 0)
-
-    def parts_left(place, carry):
-        summand(place, step_of(place + 1)).wait_send()
-        return carry
-
-    lax.fori_loop(0, blocks - 1, parts_left, 0)
+    for side in range(2):
+        for where in range(2):
+            far_part(side, where).wait_send()
+            near_part(side, where).wait_send()
+    swap.wait_send()
 
 
 def shards(velsq, epsilon, delta, tilt, azimuth, forward, adjoint, wavelet, source, receivers, observed):
@@ -470,7 +534,7 @@
         return pltpu.VMEM(lead + (planes, rows, lanes), jnp.float32)
 
     def by_block(count):
-        return pltpu.VMEM((count, 5, planes, block, lanes), jnp.float32)
+        return pltpu.VMEM(count + (planes, 5, block, lanes), jnp.float32)
 
     sems = pltpu.SemaphoreType.DMA
     return pl.pallas_call(
@@ -478,22 +542,27 @@
         out_shape=jax.ShapeDtypeStruct((5, planes, block, lanes), jnp.float32),
         in_specs=[anywhere] * 7 + [smem, smem, vmem, vmem],
         out_specs=vmem,
-        scratch_shapes=[by_block(blocks)]
+        scratch_shapes=[by_block((blocks,))]
         + [padded] * 6
-        + [fields(4), fields(9), fields(6), fields(2), fields(2), by_block(blocks), by_block(blocks - 1)]
+        + [fields(4), fields(9), fields(6), fields(2), fields(2), by_block((blocks,))]
+        + [pltpu.VMEM((2, 2, 5, block, lanes), jnp.float32), by_block((2, 2)), by_block(())]
         + [
             sems((13,)),
-            sems((blocks - 1,)),
-            sems((blocks - 1,)),
+            sems((9,)),
+            sems((10,)),
             sems((8,)),
             sems((8,)),
             sems((4 * blocks,)),
             sems((4 * blocks,)),
-            sems((blocks - 1,)),
-            sems((blocks - 1,)),
+            sems((4,)),
+            sems((4,)),
+            sems((4,)),
+            sems((4,)),
+            sems(()),
+            sems(()),
         ],
         compiler_params=pltpu.CompilerParams(
-            collective_id=0, has_side_effects=True, vmem_limit_bytes=40 << 20
+            collective_id=0, has_side_effects=True, vmem_limit_bytes=60 << 20
         ),
         name="gradient",
     )(velsq, epsilon, delta, tilt, azimuth, forward, adjoint, wavelet, source, receivers, observed)

time: 65.3 us -> 49.4 us (0.76)
  the two profiles are of different devices: /device:TPU:193 before, /device:TPU:56 now
where the time goes in v2:
time: 49.4 us; the launch traced here: 49.3 us
  Pallas kernels  47 us (95%)
  local copies, waits for them, and re-layouts  1.59 us (3%)
  between operations  0.66 us (1%)
    pallas_call x1, Pallas kernels, shards(): pl.pallas_call(kernel, out_shape=jax.ShapeDtypeStruct((5, planes, block,...  47 us
    unnamed x1, local copies, waits for them, and re-layouts  1.59 us

profile of v2, /device:TPU:56, one launch (start us, length us, event | category | flops | bytes accessed | tf_op | source)
XLA Modules:
  0.0 49.3 jit_solution(6413490827849311872)
XLA Ops:
  0.7 47.0 %gradient.1 = f32[5,2,32,128]{3,2,1,0:T(8,128)} custom-call(f32[2,32,128]{2,1,0:T(8,128)} %velsq.1, f32[2,32,128]{2,1,0:T(8,128)} %epsilon.1, f32[2,32,128]{2,1,0:T(8,128)} %delta.1, f32[2,32,128]{2,1,0:T(8,128)} %tilt.1, f32[2,32,128]{2,1,0:T(8,128)} %azimuth.1, f32[1,4,2,256,128]{4,3,2,1,0:T(8,128)} %forward.1, f32[1,4,2,256,128]{4,3,2,1,0:T(8,128)} %adjoint.1, ...), custom_call_target="tpu_custom_call" | custom-call | tf_op jit(solution)/shard_map/gradient/pallas_call | solution.py:540
  47.7 1.6 %copy.14 = f32[5,2,32,128]{3,2,1,0:T(8,128)} copy(f32[5,2,32,128]{3,2,1,0:T(8,128)} %gradient.1) | data formatting | bytes 327680

commit v3 on v2

--- a/solution.py
+++ b/solution.py
@@ -78,18 +78,18 @@
     azimuth,
     forward,
     adjoint,
+    wavelet_in,
+    source,
+    receivers_in,
+    observed_in,
+    out,
     wavelet,
-    source,
     receivers,
     observed,
-    out,
     coef,
-    pad_p,
-    pad_q,
-    pad_a,
-    pad_b,
-    pad_p1,
-    pad_q1,
+    pad_pq,
+    pad_ab,
+    pad_next,
     olds,
     table,
     terms,
@@ -116,10 +116,10 @@
     shot = lax.axis_index("shot")
     domain = lax.axis_index("domain")
     slabs = lax.axis_size("domain")
-    rows = pad_p.shape[1] - 2 * PAD
+    rows = pad_pq.shape[2] - 2 * PAD
     block = coef.shape[3]
     blocks = coef.shape[0]
-    lanes = pad_p.shape[2]
+    lanes = pad_pq.shape[3]
     has_low = domain > 0
     has_high = domain < slabs - 1
 
@@ -143,10 +143,14 @@
     for place, field in enumerate((velsq, epsilon, delta, tilt, azimuth)):
         local(field, coef.at[shot, :, place])
     inside = pl.ds(PAD, rows)
-    for pad, state, place in ((pad_p, forward, 1), (pad_q, forward, 3), (pad_a, adjoint, 1), (pad_b, adjoint, 3)):
-        local(state.at[0, place], pad.at[pl.ds(1, 2), inside])
+    for pad, state in ((pad_pq, forward), (pad_ab, adjoint)):
+        for place in range(2):
+            local(state.at[0, 2 * place + 1], pad.at[place, pl.ds(1, 2), inside])
     for place, (state, member) in enumerate(((forward, 0), (forward, 2), (adjoint, 0), (adjoint, 2))):
         local(state.at[0, member], olds.at[place])
+
+    for src, dst in ((wavelet_in, wavelet), (receivers_in, receivers), (observed_in, observed)):
+        local(src, dst)
 
     barrier = pltpu.get_barrier_semaphore()
     mate, right, left = other(0, 1), other(1, 0), other(3, 0)
@@ -161,37 +165,38 @@
     def _():
         pl.semaphore_signal(barrier, inc=1, device_id=(shot, domain + 1), device_id_type=MESH)
 
-    for pad in (pad_p, pad_q, pad_a, pad_b, pad_p1, pad_q1):
-        zero = jnp.zeros((4, PAD, lanes), jnp.float32)
-        pad[:, 0:PAD, :] = zero
-        pad[:, PAD + rows : 2 * PAD + rows, :] = zero
+    pads = (pad_pq, pad_ab, pad_next)
+    for pad in pads:
+        zero = jnp.zeros((2, 4, PAD, lanes), jnp.float32)
+        pad[:, :, 0:PAD, :] = zero
+        pad[:, :, PAD + rows : 2 * PAD + rows, :] = zero
 
     @pl.when(jnp.logical_not(has_low))
     def _():
-        for pad in (pad_p, pad_q, pad_a, pad_b, pad_p1, pad_q1):
-            pad[0, PAD : PAD + rows, :] = jnp.zeros((rows, lanes), jnp.float32)
+        for pad in pads:
+            pad[:, 0, PAD : PAD + rows, :] = jnp.zeros((2, rows, lanes), jnp.float32)
 
     @pl.when(jnp.logical_not(has_high))
     def _():
-        for pad in (pad_p, pad_q, pad_a, pad_b, pad_p1, pad_q1):
-            pad[3, PAD : PAD + rows, :] = jnp.zeros((rows, lanes), jnp.float32)
+        for pad in pads:
+            pad[:, 3, PAD : PAD + rows, :] = jnp.zeros((2, rows, lanes), jnp.float32)
 
     pl.semaphore_wait(barrier, 3 + has_low.astype(jnp.int32) + has_high.astype(jnp.int32))
 
-    def halo(src_low, src_high, pad, span, sems_send, sems_recv, low, high):
+    def halo(pad, span, send, recv, at):
         down = pltpu.make_async_remote_copy(
-            src_ref=src_low,
-            dst_ref=pad.at[3, span],
-            send_sem=sems_send.at[low],
-            recv_sem=sems_recv.at[low],
+            src_ref=pad.at[:, 1, span],
+            dst_ref=pad.at[:, 3, span],
+            send_sem=send.at[at, 0],
+            recv_sem=recv.at[at, 0],
             device_id=(shot, domain - 1),
             device_id_type=MESH,
         )
         up = pltpu.make_async_remote_copy(
-            src_ref=src_high,
-            dst_ref=pad.at[0, span],
-            send_sem=sems_send.at[high],
-            recv_sem=sems_recv.at[high],
+            src_ref=pad.at[:, 2, span],
+            dst_ref=pad.at[:, 0, span],
+            send_sem=send.at[at, 1],
+            recv_sem=recv.at[at, 1],
             device_id=(shot, domain + 1),
             device_id_type=MESH,
         )
@@ -209,13 +214,9 @@
         pl.when(has_low)(pair[0].wait_send)
         pl.when(has_high)(pair[1].wait_send)
 
-    first_halo = []
-    for place, (pad, state, member) in enumerate(
-        ((pad_p, forward, 1), (pad_q, forward, 3), (pad_a, adjoint, 1), (pad_b, adjoint, 3))
-    ):
-        first_halo.append(
-            halo(state.at[0, member, 0], state.at[0, member, 1], pad, inside, halo_send, halo_recv, 2 * place, 2 * place + 1)
-        )
+    halo_pq = halo(pad_pq, inside, halo_send, halo_recv, 0)
+    halo_ab = halo(pad_ab, inside, halo_send, halo_recv, 1)
+
     def push(part, peer, send_sem, recv_sem):
         return pltpu.make_async_remote_copy(
             src_ref=part,
@@ -229,23 +230,31 @@
     def landed(part, recv_sem):
         pltpu.make_async_copy(part, part, recv_sem).wait()
 
-    sends = [
-        push(coef.at[shot], mate, gather_send.at[0], gather_recv.at[1]),
-        push(coef.at[shot], right, gather_send.at[1], gather_recv.at[3]),
-        push(coef.at[shot], left, gather_send.at[2], gather_recv.at[2]),
-        push(coef.at[mate], right, gather_send.at[3], gather_recv.at[5]),
-        push(coef.at[mate], left, gather_send.at[4], gather_recv.at[4]),
-        push(coef.at[left, 0], right, gather_send.at[5], gather_recv.at[6]),
-        push(coef.at[right, 1], left, gather_send.at[6], gather_recv.at[7]),
-        push(coef.at[other(3, 1), 0], right, gather_send.at[7], gather_recv.at[8]),
-        push(coef.at[other(1, 1), 1], left, gather_send.at[8], gather_recv.at[9]),
-    ]
+    def own_part(plane, side):
+        return push(coef.at[shot, plane], (mate, right, left)[side], gather_send.at[3 * plane + side], gather_recv.at[plane, (1, 3, 2)[side]])
+
+    def mate_part(plane, side):
+        return push(coef.at[mate, plane], (right, left)[side], gather_send.at[6 + 2 * plane + side], gather_recv.at[plane, (5, 4)[side]])
+
+    def far_coef(where, side):
+        part = coef.at[other((3, 1)[side], where), side]
+        return push(part, (right, left)[side], gather_send.at[10 + 2 * where + side], gather_recv.at[side, 6 + where])
+
+    def pass_far(where):
+        for side in range(2):
+            owner = other((3, 1)[side], where)
+            landed(coef.at[owner, side], gather_recv.at[side, (3, 2)[side] + 2 * where])
+            far_coef(where, side).start()
+
     for copy in locals_[0:5]:
         copy.wait()
-    for copy in sends[0:3]:
-        copy.start()
-    begin(first_halo[0])
-    begin(first_halo[1])
+    for plane, side in ((0, 0), (0, 1), (1, 2), (1, 0), (1, 1), (0, 2)):
+        own_part(plane, side).start()
+    for copy in locals_[5:9]:
+        copy.wait()
+    begin(halo_pq)
+    for copy in locals_[13:]:
+        copy.wait()
 
     cells = receivers[...] - domain * (2 * rows * lanes)
     at_row = lax.shift_right_arithmetic(cells, 7)
@@ -275,27 +284,19 @@
     def at_source(row, amount):
         return jnp.where(cell == source_at - row * lanes, amount, 0.0)
 
-    landed(coef.at[mate], gather_recv.at[1])
-    sends[3].start()
-    sends[4].start()
-    landed(coef.at[left], gather_recv.at[3])
-    sends[5].start()
-    landed(coef.at[right], gather_recv.at[2])
-    sends[6].start()
-    begin(first_halo[2])
-    begin(first_halo[3])
-    for copy in locals_[5:]:
+    for plane in range(2):
+        landed(coef.at[mate, plane], gather_recv.at[plane, 1])
+        mate_part(plane, plane).start()
+        mate_part(plane, 1 - plane).start()
+    pass_far(0)
+    begin(halo_ab)
+    for copy in locals_[9:13]:
         copy.wait()
-    arrived(first_halo[0])
-    arrived(first_halo[1])
+    arrived(halo_pq)
 
     def next_halo(owner):
         span = pl.ds(pl.multiple_of(owner * block + PAD, TILE), block)
-        pairs = []
-        for place, pad in enumerate((pad_p1, pad_q1)):
-            at = (owner * 2 + place) * 2
-            pairs.append(halo(pad.at[1, span], pad.at[2, span], pad, span, next_send, next_recv, at, at + 1))
-        return pairs
+        return halo(pad_next, span, next_send, next_recv, owner)
 
     def forward_tile(owner, tile):
         inner = pl.ds(pl.multiple_of(tile * TILE, TILE), TILE)
@@ -311,8 +312,8 @@
         root = jnp.sqrt(1.0 + 2.0 * dlt)
         for place, values in enumerate(axis + turn + (stretch, root, speed)):
             table[place, :, span, :] = values
-        here_p, hess_p = hessian(pad_p, row + PAD, first, last)
-        here_q, hess_q = hessian(pad_q, row + PAD, first, last)
+        here_p, hess_p = hessian(pad_pq.at[0], row + PAD, first, last)
+        here_q, hess_q = hessian(pad_pq.at[1], row + PAD, first, last)
         lean_p = times_axis(hess_p, axis, quarter)
         lean_q = times_axis(hess_q, axis, quarter)
         across = hess_p[0] + hess_p[1] + hess_p[2] - dot3(axis, lean_p)
@@ -321,8 +322,8 @@
         drive_q = root * across + axial
         pulse = at_source(row, wavelet[0, 0])
         here = pl.ds(pl.multiple_of(row + PAD, TILE), TILE)
-        pad_p1[1:3, here, :] = 2.0 * here_p - olds[0, :, span, :] + speed * drive_p + pulse
-        pad_q1[1:3, here, :] = 2.0 * here_q - olds[1, :, span, :] + speed * drive_q + pulse
+        pad_next[0, 1:3, here, :] = 2.0 * here_p - olds[0, :, span, :] + speed * drive_p + pulse
+        pad_next[1, 1:3, here, :] = 2.0 * here_q - olds[1, :, span, :] + speed * drive_q + pulse
         for place, values in enumerate(
             (
                 across,
@@ -340,50 +341,56 @@
     def forward_block(place, carry):
         owner = step_of(place)
 
-        @pl.when(place == 3)
+        @pl.when((place == 2) | (place == 3))
         def _():
-            landed(coef.at[other(3, 1)], gather_recv.at[5])
-            sends[7].start()
-            landed(coef.at[other(1, 1)], gather_recv.at[4])
-            sends[8].start()
+            landed(coef.at[owner, place - 2], gather_recv.at[place - 2, place])
+
+        @pl.when(place == 4)
+        def _():
+            pass_far(1)
+
+        @pl.when((place == 4) | (place == 5))
+        def _():
+            landed(coef.at[owner, place - 4], gather_recv.at[place - 4, place])
 
         @pl.when(place >= 6)
         def _():
             for plane in range(2):
-                landed(coef.at[owner, plane], gather_recv.at[2 * place - 6 + plane])
+                landed(coef.at[owner, plane], gather_recv.at[plane, place])
 
         lax.fori_loop(0, tiles, lambda tile, c: (forward_tile(owner, tile), c)[1], 0)
-        for pair in next_halo(owner):
-            begin(pair)
+        begin(next_halo(owner))
         return carry
 
     lax.fori_loop(0, blocks, forward_block, 0)
 
-    arrived(first_halo[2])
-    arrived(first_halo[3])
+    arrived(halo_ab)
 
     def load_table(span):
         values = tuple(table[place, :, span, :] for place in range(9))
         return values[0:3], values[3:6], values[6], values[7], values[8]
 
-    def adjoint_tile(tile, carry):
-        row = pl.multiple_of(tile * TILE, TILE)
+    def adjoint_tile(owner, tile):
+        row = pl.multiple_of(owner * block + tile * TILE, TILE)
         span = pl.ds(row, TILE)
         axis, _, stretch, root, speed = load_table(span)
         quarter = tuple(0.25 * part for part in axis)
-        here_a, hess_a = hessian(pad_a, row + PAD, first, last)
-        here_b, hess_b = hessian(pad_b, row + PAD, first, last)
+        here_a, hess_a = hessian(pad_ab.at[0], row + PAD, first, last)
+        here_b, hess_b = hessian(pad_ab.at[1], row + PAD, first, last)
         across = hess_a[0] + hess_a[1] + hess_a[2] - dot3(axis, times_axis(hess_a, axis, quarter))
         axial = dot3(axis, times_axis(hess_b, axis, quarter))
         step_a[0, :, span, :] = 2.0 * here_a - olds[2, :, span, :] + speed * (stretch * across + root * axial)
         step_a[1, :, span, :] = 2.0 * here_b - olds[3, :, span, :] + speed * (root * across + axial)
+
+    def adjoint_block(place, carry):
+        owner = step_of(place)
+        lax.fori_loop(0, tiles, lambda tile, c: (adjoint_tile(owner, tile), c)[1], 0)
         return carry
 
-    lax.fori_loop(0, rows // TILE, adjoint_tile, 0)
+    lax.fori_loop(6, blocks, adjoint_block, 0)
 
     def halo_in(owner, carry):
-        for pair in next_halo(owner):
-            arrived(pair)
+        arrived(next_halo(owner))
         return carry
 
     lax.fori_loop(0, blocks, halo_in, 0)
@@ -394,16 +401,16 @@
         span = pl.ds(row, TILE)
         axis, turn, stretch, root, speed = load_table(span)
         quarter = tuple(0.25 * part for part in axis)
-        here_p, hess_p = hessian(pad_p1, row + PAD, first, last)
-        _, hess_q = hessian(pad_q1, row + PAD, first, last)
+        here_p, hess_p = hessian(pad_next.at[0], row + PAD, first, last)
+        _, hess_q = hessian(pad_next.at[1], row + PAD, first, last)
         lean_p = times_axis(hess_p, axis, quarter)
         lean_q = times_axis(hess_q, axis, quarter)
         across1 = hess_p[0] + hess_p[1] + hess_p[2] - dot3(axis, lean_p)
         axial1 = dot3(axis, lean_q)
         here = pl.ds(pl.multiple_of(row + PAD, TILE), TILE)
-        last_p = 2.0 * here_p - pad_p[1:3, here, :] + speed * (stretch * across1 + root * axial1)
+        last_p = 2.0 * here_p - pad_pq[0, 1:3, here, :] + speed * (stretch * across1 + root * axial1)
         last_p = last_p + at_source(row, wavelet[0, 1])
-        late_a, late_b = pad_a[1:3, here, :], pad_b[1:3, here, :]
+        late_a, late_b = pad_ab[0, 1:3, here, :], pad_ab[1, 1:3, here, :]
         early_a = step_a[0, :, span, :] + (hits[0, :, span, :] * last_p - hits[1, :, span, :])
         early_b = step_a[1, :, span, :]
         across0, axial0, tilt_p0, tilt_q0, spin_p0, spin_q0 = (terms[place, :, span, :] for place in range(6))
@@ -443,12 +450,12 @@
             device_id_type=MESH,
         )
 
-    def near_part(side, where):
+    def near_part(side, where, plane):
         return pltpu.make_async_remote_copy(
-            src_ref=grad.at[other((1, 3)[side], where)],
-            dst_ref=near.at[side, where],
-            send_sem=near_send.at[2 * side + where],
-            recv_sem=near_recv.at[2 * side + where],
+            src_ref=grad.at[other((1, 3)[side], where), plane],
+            dst_ref=near.at[side, where, plane],
+            send_sem=near_send.at[4 * side + 2 * where + plane],
+            recv_sem=near_recv.at[4 * side + 2 * where + plane],
             device_id=((right, left)[side], domain),
             device_id_type=MESH,
         )
@@ -458,7 +465,7 @@
             owner = other((1, 3)[side], where)
             far_part(side, where).wait_recv()
             grad[owner, side] = grad[owner, side] + far[side, where]
-            near_part(side, where).start()
+            near_part(side, where, side).start()
 
     def gradient_block(turn_at, carry):
         place = jnp.where(
@@ -467,6 +474,11 @@
             jnp.where(turn_at < 4, turn_at + 2, jnp.where(turn_at < 6, turn_at - 2, 7 - turn_at)),
         )
         owner = step_of(place)
+
+        @pl.when(turn_at == 2)
+        def _():
+            lax.fori_loop(0, 6, adjoint_block, 0)
+
         lax.fori_loop(0, tiles, lambda tile, c: (gradient_tile(owner, tile), c)[1], 0)
         for where in range(2):
 
@@ -474,6 +486,12 @@
             def _():
                 for side in range(2):
                     far_part(side, where).start()
+
+            for side in range(2):
+
+                @pl.when(turn_at == 4 - 2 * where + side)
+                def _():
+                    near_part(side, where, 1 - side).start()
 
             @pl.when(turn_at == 5 - 2 * where)
             def _():
@@ -491,33 +509,40 @@
         device_id=(mate, domain),
         device_id_type=MESH,
     )
+    for plane in range(2):
+        for side in range(3):
+            own_part(plane, side).wait_send()
+        for side in range(2):
+            mate_part(plane, side).wait_send()
+            far_coef(plane, side).wait_send()
+    sent(halo_pq)
+    sent(halo_ab)
+
+    def drained(owner, carry):
+        sent(next_halo(owner))
+        return carry
+
+    lax.fori_loop(0, blocks, drained, 0)
+
     for side in range(2):
-        near_part(side, 1).wait_recv()
+        for plane in range(2):
+            near_part(side, 1, plane).wait_recv()
     grad[mate] = grad[mate] + (near[0, 1] + near[1, 1])
     swap.start()
     for side in range(2):
-        near_part(side, 0).wait_recv()
+        for plane in range(2):
+            near_part(side, 0, plane).wait_recv()
     total = grad[shot] + (near[0, 0] + near[1, 0])
     swap.wait_recv()
     total = total + mates[...]
     for plane in range(2):
         out[:, plane] = total[plane]
 
-    for copy in sends:
-        copy.wait_send()
-    for pair in first_halo:
-        sent(pair)
-
-    def drained(owner, carry):
-        for pair in next_halo(owner):
-            sent(pair)
-        return carry
-
-    lax.fori_loop(0, blocks, drained, 0)
     for side in range(2):
         for where in range(2):
             far_part(side, where).wait_send()
-            near_part(side, where).wait_send()
+            for plane in range(2):
+                near_part(side, where, plane).wait_send()
     swap.wait_send()
 
 
@@ -525,10 +550,9 @@
     planes, block, lanes = velsq.shape
     rows = forward.shape[3]
     blocks = rows // block
-    padded = pltpu.VMEM((planes + 2, rows + 2 * PAD, lanes), jnp.float32)
+    padded = pltpu.VMEM((2, planes + 2, rows + 2 * PAD, lanes), jnp.float32)
     anywhere = pl.BlockSpec(memory_space=pl.ANY)
     vmem = pl.BlockSpec(memory_space=pltpu.VMEM)
-    smem = pl.BlockSpec(memory_space=pltpu.SMEM)
 
     def fields(*lead):
         return pltpu.VMEM(lead + (planes, rows, lanes), jnp.float32)
@@ -537,35 +561,41 @@
         return pltpu.VMEM(count + (planes, 5, block, lanes), jnp.float32)
 
     sems = pltpu.SemaphoreType.DMA
+    held = [
+        pltpu.with_memory_space_constraint(values, pltpu.HBM)
+        for values in (velsq, epsilon, delta, tilt, azimuth, forward, adjoint, wavelet, receivers, observed)
+    ]
     return pl.pallas_call(
         kernel,
         out_shape=jax.ShapeDtypeStruct((5, planes, block, lanes), jnp.float32),
-        in_specs=[anywhere] * 7 + [smem, smem, vmem, vmem],
+        in_specs=[anywhere] * 8 + [pl.BlockSpec(memory_space=pltpu.SMEM)] + [anywhere] * 2,
         out_specs=vmem,
-        scratch_shapes=[by_block((blocks,))]
-        + [padded] * 6
+        scratch_shapes=[pltpu.SMEM(wavelet.shape, jnp.float32)]
+        + [pltpu.VMEM(receivers.shape, jnp.int32), pltpu.VMEM(observed.shape, jnp.float32)]
+        + [by_block((blocks,))]
+        + [padded] * 3
         + [fields(4), fields(9), fields(6), fields(2), fields(2), by_block((blocks,))]
         + [pltpu.VMEM((2, 2, 5, block, lanes), jnp.float32), by_block((2, 2)), by_block(())]
         + [
-            sems((13,)),
-            sems((9,)),
-            sems((10,)),
+            sems((16,)),
+            sems((14,)),
+            sems((2, blocks)),
+            sems((2, 2)),
+            sems((2, 2)),
+            sems((blocks, 2)),
+            sems((blocks, 2)),
+            sems((4,)),
+            sems((4,)),
             sems((8,)),
             sems((8,)),
-            sems((4 * blocks,)),
-            sems((4 * blocks,)),
-            sems((4,)),
-            sems((4,)),
-            sems((4,)),
-            sems((4,)),
             sems(()),
             sems(()),
         ],
         compiler_params=pltpu.CompilerParams(
-            collective_id=0, has_side_effects=True, vmem_limit_bytes=60 << 20
+            collective_id=0, has_side_effects=True, vmem_limit_bytes=40 << 20
         ),
         name="gradient",
-    )(velsq, epsilon, delta, tilt, azimuth, forward, adjoint, wavelet, source, receivers, observed)
+    )(*held[:8], source, *held[8:])
 
 
 def solution(mesh):

time: 49.4 us -> 46.7 us (0.945)
  the two profiles are of different devices: /device:TPU:56 before, /device:TPU:176 now
where the time goes in v3:
time: 46.7 us; the launch traced here: 46.6 us
  Pallas kernels  45.3 us (97%)
  local copies, waits for them, and re-layouts  0.67 us (1%)
  between operations  0.66 us (1%)
    pallas_call x1, Pallas kernels, shards(): pl.pallas_call(kernel, out_shape=jax.ShapeDtypeStruct((5, planes, block,...  45.3 us

profile of v3, /device:TPU:176, one launch (start us, length us, event | category | flops | bytes accessed | tf_op | source)
XLA Modules:
  0.0 46.6 jit_solution(17851805853608115926)
XLA Ops:
  0.7 45.3 %gradient.1 = f32[5,2,32,128]{3,2,1,0:T(8,128)S(1)} custom-call(f32[2,32,128]{2,1,0:T(8,128)} %velsq.1, f32[2,32,128]{2,1,0:T(8,128)} %epsilon.1, f32[2,32,128]{2,1,0:T(8,128)} %delta.1, f32[2,32,128]{2,1,0:T(8,128)} %tilt.1, f32[2,32,128]{2,1,0:T(8,128)} %azimuth.1, f32[1,4,2,256,128]{4,3,2,1,0:T(8,128)} %forward.1, f32[1,4,2,256,128]{4,3,2,1,0:T(8,128)} %adjoint.1, ...), custom_call_target="tpu_custom_call" | custom-call | tf_op jit(solution)/shard_map/gradient/pallas_call | solution.py:568
  45.9 0.7 %copy.14 = f32[5,2,32,128]{3,2,1,0:T(8,128)} copy(f32[5,2,32,128]{3,2,1,0:T(8,128)S(1)} %gradient.1) | data formatting | bytes 327680

commit v4 on v3

--- a/solution.py
+++ b/solution.py
@@ -215,7 +215,14 @@
         pl.when(has_high)(pair[1].wait_send)
 
     halo_pq = halo(pad_pq, inside, halo_send, halo_recv, 0)
-    halo_ab = halo(pad_ab, inside, halo_send, halo_recv, 1)
+    window = 2 * block
+
+    def piece(step, offset, size, at):
+        row = pl.multiple_of(lax.rem(shot // 2 + step, 4) * window + offset + PAD, TILE)
+        return halo(pad_ab, pl.ds(row, size), halo_send, halo_recv, at)
+
+    halo_ab = (piece(2, 0, window, 1), piece(3, 0, TILE, 2), piece(1, window - TILE, TILE, 3))
+    halo_ab_late = (piece(1, 0, window - TILE, 4), piece(3, TILE, window - TILE, 5), piece(0, 0, window, 6))
 
     def push(part, peer, send_sem, recv_sem):
         return pltpu.make_async_remote_copy(
@@ -289,7 +296,8 @@
         mate_part(plane, plane).start()
         mate_part(plane, 1 - plane).start()
     pass_far(0)
-    begin(halo_ab)
+    for pair in halo_ab:
+        begin(pair)
     for copy in locals_[9:13]:
         copy.wait()
     arrived(halo_pq)
@@ -358,13 +366,22 @@
             for plane in range(2):
                 landed(coef.at[owner, plane], gather_recv.at[plane, place])
 
-        lax.fori_loop(0, tiles, lambda tile, c: (forward_tile(owner, tile), c)[1], 0)
-        begin(next_halo(owner))
+        lax.fori_loop(0, tiles, lambda tile, c: (forward_tile(owner, tile), c)[1], 0, unroll=4)
+
+        @pl.when(place >= 2)
+        def _():
+            begin(next_halo(owner))
+
         return carry
 
     lax.fori_loop(0, blocks, forward_block, 0)
 
-    arrived(halo_ab)
+    for place in range(2):
+        begin(next_halo(step_of(place)))
+    for pair in halo_ab_late:
+        begin(pair)
+    for pair in halo_ab:
+        arrived(pair)
 
     def load_table(span):
         values = tuple(table[place, :, span, :] for place in range(9))
@@ -384,16 +401,16 @@
 
     def adjoint_block(place, carry):
         owner = step_of(place)
-        lax.fori_loop(0, tiles, lambda tile, c: (adjoint_tile(owner, tile), c)[1], 0)
+        lax.fori_loop(0, tiles, lambda tile, c: (adjoint_tile(owner, tile), c)[1], 0, unroll=4)
         return carry
 
     lax.fori_loop(6, blocks, adjoint_block, 0)
 
-    def halo_in(owner, carry):
-        arrived(next_halo(owner))
-        return carry
-
-    lax.fori_loop(0, blocks, halo_in, 0)
+    def halo_in(steps):
+        for step, y in steps:
+            arrived(next_halo(lax.rem(shot // 2 + step, 4) * 2 + y))
+
+    halo_in(((2, 0), (2, 1), (1, 1), (3, 0)))
 
     def gradient_tile(owner, tile):
         inner = pl.ds(pl.multiple_of(tile * TILE, TILE), TILE)
@@ -477,9 +494,15 @@
 
         @pl.when(turn_at == 2)
         def _():
-            lax.fori_loop(0, 6, adjoint_block, 0)
-
-        lax.fori_loop(0, tiles, lambda tile, c: (gradient_tile(owner, tile), c)[1], 0)
+            halo_in(((1, 0), (3, 1), (0, 0), (0, 1)))
+            for pair in halo_ab_late:
+                arrived(pair)
+
+        @pl.when(turn_at >= 2)
+        def _():
+            adjoint_block(place, 0)
+
+        lax.fori_loop(0, tiles, lambda tile, c: (gradient_tile(owner, tile), c)[1], 0, unroll=4)
         for where in range(2):
 
             @pl.when(turn_at == 1 - where)
@@ -516,7 +539,8 @@
             mate_part(plane, side).wait_send()
             far_coef(plane, side).wait_send()
     sent(halo_pq)
-    sent(halo_ab)
+    for pair in halo_ab + halo_ab_late:
+        sent(pair)
 
     def drained(owner, carry):
         sent(next_halo(owner))
@@ -580,8 +604,8 @@
             sems((16,)),
             sems((14,)),
             sems((2, blocks)),
-            sems((2, 2)),
-            sems((2, 2)),
+            sems((7, 2)),
+            sems((7, 2)),
             sems((blocks, 2)),
             sems((blocks, 2)),
             sems((4,)),

time: 46.7 us -> 44.7 us (0.957)
  the two profiles are of different devices: /device:TPU:176 before, /device:TPU:48 now
where the time goes in v4:
time: 44.7 us; the launch traced here: 44.6 us
  Pallas kernels  43.3 us (97%)
  local copies, waits for them, and re-layouts  0.67 us (1%)
  between operations  0.66 us (1%)
    pallas_call x1, Pallas kernels, shards(): pl.pallas_call(kernel, out_shape=jax.ShapeDtypeStruct((5, planes, block,...  43.3 us

profile of v4, /device:TPU:48, one launch (start us, length us, event | category | flops | bytes accessed | tf_op | source)
XLA Modules:
  0.0 44.6 jit_solution(6115192088641657129)
XLA Ops:
  0.7 43.3 %gradient.1 = f32[5,2,32,128]{3,2,1,0:T(8,128)S(1)} custom-call(f32[2,32,128]{2,1,0:T(8,128)} %velsq.1, f32[2,32,128]{2,1,0:T(8,128)} %epsilon.1, f32[2,32,128]{2,1,0:T(8,128)} %delta.1, f32[2,32,128]{2,1,0:T(8,128)} %tilt.1, f32[2,32,128]{2,1,0:T(8,128)} %azimuth.1, f32[1,4,2,256,128]{4,3,2,1,0:T(8,128)} %forward.1, f32[1,4,2,256,128]{4,3,2,1,0:T(8,128)} %adjoint.1, ...), custom_call_target="tpu_custom_call" | custom-call | tf_op jit(solution)/shard_map/gradient/pallas_call | solution.py:592
  43.9 0.7 %copy.14 = f32[5,2,32,128]{3,2,1,0:T(8,128)} copy(f32[5,2,32,128]{3,2,1,0:T(8,128)S(1)} %gradient.1) | data formatting | bytes 327680

commit v5 on v4

--- a/solution.py
+++ b/solution.py
@@ -346,7 +346,8 @@
 
     tiles = block // TILE
 
-    def forward_block(place, carry):
+    def forward_block(turn_at, carry):
+        place = jnp.where(turn_at < 2, turn_at + 2, jnp.where(turn_at < 4, turn_at - 2, turn_at))
         owner = step_of(place)
 
         @pl.when((place == 2) | (place == 3))

time: 44.7 us -> 44.3 us (level)
  no operation moved by 1% of the time
where the time goes in v5:
time: 44.3 us; the launch traced here: 44.2 us
  Pallas kernels  42.9 us (97%)
  local copies, waits for them, and re-layouts  0.67 us (2%)
  between operations  0.66 us (1%)
    pallas_call x1, Pallas kernels, shards(): pl.pallas_call(kernel, out_shape=jax.ShapeDtypeStruct((5, planes, block,...  42.9 us

profile of v5, /device:TPU:48, one launch (start us, length us, event | category | flops | bytes accessed | tf_op | source)
XLA Modules:
  0.0 44.2 jit_solution(17157422504717227253)
XLA Ops:
  0.7 42.9 %gradient.1 = f32[5,2,32,128]{3,2,1,0:T(8,128)S(1)} custom-call(f32[2,32,128]{2,1,0:T(8,128)} %velsq.1, f32[2,32,128]{2,1,0:T(8,128)} %epsilon.1, f32[2,32,128]{2,1,0:T(8,128)} %delta.1, f32[2,32,128]{2,1,0:T(8,128)} %tilt.1, f32[2,32,128]{2,1,0:T(8,128)} %azimuth.1, f32[1,4,2,256,128]{4,3,2,1,0:T(8,128)} %forward.1, f32[1,4,2,256,128]{4,3,2,1,0:T(8,128)} %adjoint.1, ...), custom_call_target="tpu_custom_call" | custom-call | tf_op jit(solution)/shard_map/gradient/pallas_call | solution.py:593
  43.5 0.7 %copy.14 = f32[5,2,32,128]{3,2,1,0:T(8,128)} copy(f32[5,2,32,128]{3,2,1,0:T(8,128)S(1)} %gradient.1) | data formatting | bytes 327680

commit v6 on v5

--- a/solution.py
+++ b/solution.py
@@ -525,14 +525,16 @@
 
     lax.fori_loop(0, blocks, gradient_block, 0)
 
-    swap = pltpu.make_async_remote_copy(
-        src_ref=grad.at[mate],
-        dst_ref=mates,
-        send_sem=mate_send,
-        recv_sem=mate_recv,
-        device_id=(mate, domain),
-        device_id_type=MESH,
-    )
+    def swap(plane):
+        return pltpu.make_async_remote_copy(
+            src_ref=grad.at[mate, plane],
+            dst_ref=mates.at[plane],
+            send_sem=mate_send.at[plane],
+            recv_sem=mate_recv.at[plane],
+            device_id=(mate, domain),
+            device_id_type=MESH,
+        )
+
     for plane in range(2):
         for side in range(3):
             own_part(plane, side).wait_send()
@@ -549,26 +551,26 @@
 
     lax.fori_loop(0, blocks, drained, 0)
 
-    for side in range(2):
-        for plane in range(2):
+    for plane in range(2):
+        for side in range(2):
             near_part(side, 1, plane).wait_recv()
-    grad[mate] = grad[mate] + (near[0, 1] + near[1, 1])
-    swap.start()
+        grad[mate, plane] = grad[mate, plane] + (near[0, 1, plane] + near[1, 1, plane])
+        swap(plane).start()
     for side in range(2):
         for plane in range(2):
             near_part(side, 0, plane).wait_recv()
     total = grad[shot] + (near[0, 0] + near[1, 0])
-    swap.wait_recv()
-    total = total + mates[...]
     for plane in range(2):
-        out[:, plane] = total[plane]
+        swap(plane).wait_recv()
+        out[:, plane] = total[plane] + mates[plane]
 
     for side in range(2):
         for where in range(2):
             far_part(side, where).wait_send()
             for plane in range(2):
                 near_part(side, where, plane).wait_send()
-    swap.wait_send()
+    for plane in range(2):
+        swap(plane).wait_send()
 
 
 def shards(velsq, epsilon, delta, tilt, azimuth, forward, adjoint, wavelet, source, receivers, observed):
@@ -613,8 +615,8 @@
             sems((4,)),
             sems((8,)),
             sems((8,)),
-            sems(()),
-            sems(()),
+            sems((2,)),
+            sems((2,)),
         ],
         compiler_params=pltpu.CompilerParams(
             collective_id=0, has_side_effects=True, vmem_limit_bytes=40 << 20

time: 44.3 us -> 44.3 us (level)
  no operation moved by 1% of the time
where the time goes in v6:
time: 44.3 us; the launch traced here: 44.2 us
  Pallas kernels  42.9 us (97%)
  local copies, waits for them, and re-layouts  0.67 us (2%)
  between operations  0.66 us (1%)
    pallas_call x1, Pallas kernels, shards(): pl.pallas_call(kernel, out_shape=jax.ShapeDtypeStruct((5, planes, block,...  42.9 us

profile of v6, /device:TPU:48, one launch (start us, length us, event | category | flops | bytes accessed | tf_op | source)
XLA Modules:
  0.0 44.2 jit_solution(7237657326881574753)
XLA Ops:
  0.7 42.9 %gradient.1 = f32[5,2,32,128]{3,2,1,0:T(8,128)S(1)} custom-call(f32[2,32,128]{2,1,0:T(8,128)} %velsq.1, f32[2,32,128]{2,1,0:T(8,128)} %epsilon.1, f32[2,32,128]{2,1,0:T(8,128)} %delta.1, f32[2,32,128]{2,1,0:T(8,128)} %tilt.1, f32[2,32,128]{2,1,0:T(8,128)} %azimuth.1, f32[1,4,2,256,128]{4,3,2,1,0:T(8,128)} %forward.1, f32[1,4,2,256,128]{4,3,2,1,0:T(8,128)} %adjoint.1, ...), custom_call_target="tpu_custom_call" | custom-call | tf_op jit(solution)/shard_map/gradient/pallas_call | solution.py:595
  43.5 0.7 %copy.14 = f32[5,2,32,128]{3,2,1,0:T(8,128)} copy(f32[5,2,32,128]{3,2,1,0:T(8,128)S(1)} %gradient.1) | data formatting | bytes 327680
